TPU v7x, 32 devices: a whole 2x2x4 slice. The times are simulated.
32 devices in a mesh: blk: 8 (over z, y), lblk: 4 (over x, core).
Axes of the slice: x: 2, y: 2, z: 4, core: 2. Of those that a mesh axis runs over, the one named last changes fastest.
Arguments:
- sky: bfloat16 [8, 2, 32, 16384], P(None, None, 'blk', 'lblk'), may hold values from -6 to 6
- arc_start: int32 [2, 32], P(None, 'blk'), may hold values from 0 to 16383
- arc_count: int32 [2, 32], P(None, 'blk'), may hold values from 4096 to 16384
- owner_modes: int32 [32], replicated, may hold values from 0 to 31, each once
- legendre: bfloat16 [32, 8, 4, 4096], P('blk', None, None, 'lblk'), may hold values from -1 to 1
Outputs:
- alm: float32 [8, 2, 32, 4096], P(None, None, 'blk', 'lblk')
Inputs may be any that keep to these rules, and one draw needn't show every extreme that they name: `owner_modes`: each m-mode 0 to 31 appears exactly once.
All inputs are finite; a program needn't handle non-finite values.
Results may differ from a plain program's by a relative error of at most 0.0049.
Values may be sent and summed in bfloat16 or wider, within the bound.
No kernel may reach another device: no remote copies, remote signals or barrier semaphores. Data moves between devices by JAX's collectives and lax.ppermute only.
A program may use at most 64 MiB of HBM per device.

v0:
```python
import math

import jax
import jax.numpy as jnp
from jax import lax
from jax.sharding import PartitionSpec as P

RLEN = 16384


DIFFUSION = 0.2


def padded(x, sides, width, wrap):
    for axis, dim in sides:
        count, length = (lax.axis_size(axis), x.shape[dim])
        up = [(i, (i + 1) % count) for i in range(count if wrap else count - 1)]
        down = [(j, i) for i, j in up]
        last = lax.slice_in_dim(x, length - width, length, axis=dim)
        initial = lax.slice_in_dim(x, 0, width, axis=dim)
        before = lax.ppermute(last, axis, up)
        after = lax.ppermute(initial, axis, down)
        x = jnp.concatenate([before, x, after], axis=dim)
    return x


def mode_basis(positions, mode_list):
    product_index = jnp.mod(positions[:, None] * mode_list[None, :], RLEN)
    angles = 2.0 * math.pi / RLEN * product_index.astype(jnp.float32)
    return (jnp.cos(angles).astype(jnp.bfloat16), (-jnp.sin(angles)).astype(jnp.bfloat16))


def legendre_section(fourier, legendre_rows, my_modes, degrees):
    north_part = fourier[:, 0].astype(jnp.float32)
    south_part = fourier[:, 1].astype(jnp.float32)
    folded = jnp.concatenate([north_part + south_part, north_part - south_part], axis=2).astype(
        jnp.bfloat16
    )
    latitude_sums = jnp.einsum(
        "xrys,srl->xysl", folded, legendre_rows, preferred_element_type=jnp.float32
    )
    even_parity = jnp.mod(degrees[None, :] + my_modes[:, None], 2) == 0
    chosen = jnp.where(even_parity[None, None], latitude_sums[:, :2], latitude_sums[:, 2:])
    inside = (degrees[None, :] >= my_modes[:, None])[None, None]
    return jnp.where(inside, chosen, jnp.zeros((), jnp.float32))


def local(sky, arc_start, arc_count, owner_modes, legendre):
    maps_here = sky.shape[0]
    band_here = sky.shape[2]
    quarter = sky.shape[3]
    column = lax.axis_index("lblk")
    positions = column * quarter + jnp.arange(quarter, dtype=jnp.int32)
    offset = jnp.mod(positions[None, None, :] - arc_start[:, :, None], RLEN)
    kept_mask = offset < arc_count[:, :, None]
    masked = jnp.where(kept_mask[None], sky, jnp.zeros((), jnp.bfloat16))
    layered = padded(masked, (("blk", 2),), 1, False)
    edge_padded = padded(masked, (("lblk", 3),), 1, True)
    is_last = lax.axis_index("blk") == lax.axis_size("blk") - 1
    beyond = jnp.where(is_last, masked[:, ::-1, band_here - 1 :], layered[:, :, band_here + 1 :])
    centre = masked.astype(jnp.float32)
    layer_above = layered[:, :, :band_here].astype(jnp.float32)
    layer_below = jnp.concatenate([layered[:, :, 2 : band_here + 1], beyond], axis=2).astype(
        jnp.float32
    )
    pixel_before = edge_padded[:, :, :, :quarter].astype(jnp.float32)
    pixel_after = edge_padded[:, :, :, 2:].astype(jnp.float32)
    total = layer_above + layer_below + pixel_before + pixel_after - 4.0 * centre
    smooth = (centre + DIFFUSION * total).astype(jnp.bfloat16)
    cos_table, sin_table = mode_basis(positions, owner_modes)
    slab_size = owner_modes.shape[0]
    flat_rows = smooth.reshape(maps_here * 2 * band_here, quarter)
    real_part = jnp.dot(flat_rows, cos_table, preferred_element_type=jnp.float32).reshape(
        maps_here, 2, band_here, slab_size
    )
    imag_part = jnp.dot(flat_rows, sin_table, preferred_element_type=jnp.float32).reshape(
        maps_here, 2, band_here, slab_size
    )
    parity = jnp.arange(band_here, dtype=jnp.int32) % 2
    phase_turn = math.pi / RLEN * (parity[:, None] * owner_modes[None, :]).astype(jnp.float32)
    turn_cos = jnp.cos(phase_turn)
    turn_sin = jnp.sin(phase_turn)
    norm_scale = 1.0 / math.sqrt(RLEN)
    rotated_real = (real_part * turn_cos + imag_part * turn_sin) * norm_scale
    rotated_imag = (imag_part * turn_cos - real_part * turn_sin) * norm_scale
    partial_value = jnp.stack([rotated_real, rotated_imag], axis=3)
    owned_count = legendre.shape[0]
    degree_part = legendre.shape[3]
    my_modes = lax.dynamic_slice_in_dim(
        owner_modes, lax.axis_index("blk") * owned_count, owned_count
    )
    degrees = column * degree_part + jnp.arange(degree_part, dtype=jnp.int32)
    legendre_rows = legendre.reshape(owned_count, -1, degree_part)
    spread = lax.all_to_all(partial_value, "blk", split_axis=4, concat_axis=2, tiled=True)
    summed = lax.psum(spread, "lblk")
    fourier = summed.astype(jnp.bfloat16)
    result = legendre_section(fourier, legendre_rows, my_modes, degrees)
    return result


def solution(mesh):
    return jax.shard_map(
        local,
        mesh=mesh,
        in_specs=(
            P(None, None, "blk", "lblk"),
            P(None, "blk"),
            P(None, "blk"),
            P(),
            P("blk", None, None, "lblk"),
        ),
        out_specs=P(None, None, "blk", "lblk"),
        check_vma=False,
    )
```

profile of v0, /device:TPU:0, one launch (start us, length us, event | category | flops | bytes accessed | tf_op | source)
XLA Modules:
  0.0 53.8 jit_solution(13409327666316147105)
XLA Ops:
  0.0 0.7 %copy-done.1 = s32[2,4]{1,0:T(2,128)S(1)} copy-done((s32[2,4]{1,0:T(2,128)S(1)}, s32[2,4]{1,0:T(2,128)}, u32[]{:S(2)}) %copy-start.1) | copy-done | bytes 56
  0.7 0.2 fusion.16
  0.9 1.3 %broadcast_select_fusion.1 = bf16[8,2,4,4096]{3,2,1,0:T(4,128)(2,1)S(1)} fusion(bf16[8,2,4,4096]{3,2,1,0:T(4,128)(2,1)} %param.5, pred[2,4,4096]{2,1,0:T(4,128)(4,1)S(1)} %fusion.16), kind=kLoop, calls=%fused_computation.20 | loop fusion | flops 262144 | bytes 1081344 | tf_op jit(solution)/shard_map/jit(_where)/select_n | solution.py:56
  2.2 0.6 %fusion.38 = (bf16[8,2,1,4096]{3,2,1,0:T(2,128)(2,1)S(1)}, bf16[8,2,1,4096]{3,2,1,0:T(2,128)(2,1)S(1)}) fusion(bf16[8,2,4,4096]{3,2,1,0:T(4,128)(2,1)S(1)} %broadcast_select_fusion.1), kind=kLoop, calls=%fused_computation.70 | loop fusion | bytes 524288 | tf_op jit(solution)/shard_map/slice | solution.py:20
  2.8 1.3 %collective-permute-start.1 = (bf16[8,2,1,4096]{3,2,1,0:T(2,128)(2,1)S(1)}, bf16[8,2,1,4096]{3,2,1,0:T(2,128)(2,1)S(1)}, u32[]{:S(2)}, u32[]{:S(2)}) collective-permute-start(bf16[8,2,1,4096]{3,2,1,0:T(2,128)(2,1)S(1)} %get-tuple-element.5), channel_id=1, source_target_pairs={{4,0},{8,4},{12,8},{16,12},{20,16},{24,20},{28,24},{5,1},{9,5},{13... | collective-permute-start | bytes 393224 | tf_op jit(solution)/shard_map/ppermute | solution.py:22
  4.1 5.5 %collective-permute-start = (bf16[8,2,1,4096]{3,2,1,0:T(2,128)(2,1)S(1)}, bf16[8,2,1,4096]{3,2,1,0:T(2,128)(2,1)S(1)}, u32[]{:S(2)}, u32[]{:S(2)}) collective-permute-start(bf16[8,2,1,4096]{3,2,1,0:T(2,128)(2,1)S(1)} %get-tuple-element.6), channel_id=1, source_target_pairs={{0,4},{4,8},{8,12},{12,16},{16,20},{20,24},{24,28},{1,5},{5,9},{9,... | collective-permute-start | bytes 393224 | tf_op jit(solution)/shard_map/ppermute | solution.py:21
  9.8 1.7 %collective-permute-start.3 = (bf16[8,2,4,1]{3,2,1,0:T(4,128)(2,1)S(1)}, bf16[8,2,4,1]{3,2,1,0:T(4,128)(2,1)S(1)}, u32[]{:S(2)}, u32[]{:S(2)}) collective-permute-start(bf16[8,2,4,1]{3,2,1,0:T(4,128)(2,1)S(1)} %get-tuple-element.8), channel_id=1, source_target_pairs={{1,0},{2,1},{3,2},{0,3},{5,4},{6,5},{7,6},{4,7},{9,8},{10,9},{11,1... | collective-permute-start | bytes 392 | tf_op jit(solution)/shard_map/ppermute | solution.py:22
  11.6 0.3 slice.52
  12.0 2.0 %collective-permute-done.1 = bf16[8,2,1,4096]{3,2,1,0:T(2,128)(2,1)S(1)} collective-permute-done((bf16[8,2,1,4096]{3,2,1,0:T(2,128)(2,1)S(1)}, bf16[8,2,1,4096]{3,2,1,0:T(2,128)(2,1)S(1)}, u32[]{:S(2)}, u32[]{:S(2)}) %collective-permute-start.1) | collective-permute-done | bytes 131104 | tf_op jit(solution)/shard_map/ppermute | solution.py:22
  14.0 0.4 broadcast_select_fusion
  14.4 5.3 %collective-permute-done = bf16[8,2,1,4096]{3,2,1,0:T(2,128)(2,1)S(1)} collective-permute-done((bf16[8,2,1,4096]{3,2,1,0:T(2,128)(2,1)S(1)}, bf16[8,2,1,4096]{3,2,1,0:T(2,128)(2,1)S(1)}, u32[]{:S(2)}, u32[]{:S(2)}) %collective-permute-start) | collective-permute-done | bytes 131104 | tf_op jit(solution)/shard_map/ppermute | solution.py:21
  19.7 2.3 %fusion.2 = bf16[8,2,4,4096]{3,2,1,0:T(4,128)(2,1)S(1)} fusion(bf16[8,2,4,4096]{3,2,1,0:T(4,128)(2,1)S(1)} %broadcast_select_fusion.1, bf16[8,2,4,1]{3,2,1,0:T(4,128)(2,1)S(1)} %collective-permute-done.3, bf16[8,2,4,1]{3,2,1,0:T(4,128)(2,1)S(1)} %collective-permute-done.2, bf16[8,2,1,4096]{3,2,1,0:T(2,128)(2,1)S(1)} %collective-permute-done, ...), kind=kLoop, calls=%fused_computation.5 | loop fusion | flops 6553600 | bytes 1704192 | tf_op jit(solution)/shard_map/convert_element_type | solution.py:69
  22.0 2.2 %fusion.7 = f32[8,2,4,32]{3,2,1,0:T(4,128)S(1)} fusion(bf16[8,2,4,4096]{3,2,1,0:T(4,128)(2,1)S(1)} %fusion.2, s32[32]{0:T(128)S(1)} %copy-done.3, s32[4096]{0:T(1024)S(1)} %iota_add_fusion), kind=kOutput, calls=%fused_computation.22 | convolution fusion | flops 18743296 | bytes 548992 | tf_op jit(solution)/shard_map/dot_general | solution.py:73
  24.3 2.3 %multiply_bitcast_fusion.1 = (f32[8,2,4,1,32]{4,2,1,0,3:T(4,128)S(1)}, f32[8,2,4,1,32]{4,2,1,0,3:T(4,128)S(1)}) fusion(f32[8,2,4,32]{3,2,1,0:T(4,128)S(1)} %fusion.7, f32[4,32]{1,0:T(4,128)S(1)} %get-tuple-element.16, f32[4,32]{1,0:T(4,128)S(1)} %get-tuple-element.15, bf16[8,2,4,4096]{3,2,1,0:T(4,128)(2,1)S(1)} %fusion.2, s32[32]{0:T(128)S(1)} %copy-done.3, ...), kind=kOutput, calls=%fused_computation.44 | convolution fusion | flops 18890752 | bytes 566400 | tf_op jit(solution)/shard_map/dot_general | solution.py:76
  26.6 0.2 copy.16
  26.8 0.9 %reshape.175 = f32[8,1,512]{2,1,0:T(1,128)} reshape(f32[32,2,2,4,8]{4,3,2,1,0:T(4,128)S(1)} %bitcast.33) | data formatting | bytes 32768
  27.7 5.8 %all-to-all-start = ((f32[8,1,512]{2,1,0:T(1,128)}), f32[8,1,512]{2,1,0:T(1,128)S(1)}, u32[]{:S(2)}, u32[]{:S(2)}) async-start(f32[8,1,512]{2,1,0:T(1,128)} %reshape.175), calls=%async_computation | async-start | bytes 32768 | tf_op jit(solution)/shard_map/all_to_all | solution.py:94
  33.6 6.4 %all-to-all-done = f32[8,1,512]{2,1,0:T(1,128)S(1)} async-done(((f32[8,1,512]{2,1,0:T(1,128)}), f32[8,1,512]{2,1,0:T(1,128)S(1)}, u32[]{:S(2)}, u32[]{:S(2)}) %all-to-all-start) | async-done | bytes 16416 | tf_op jit(solution)/shard_map/all_to_all | solution.py:94
  40.0 0.5 broadcast.207
  40.5 0.7 %reduce = f32[8,512]{1,0:T(8,128)S(1)} reduce(f32[8,1,512]{2,1,0:T(1,128)S(1)} %all-to-all-done, f32[]{:T(128)} %broadcast.207), dimensions={1}, to_apply=%all_to_all.13.reduce_sub_computation | reduce | bytes 32772 | tf_op jit(solution)/shard_map/all_to_all | solution.py:94
  41.2 0.3 reshape.176
  42.0 10.7 %psum.7 = bf16[8,2,32,2,4]{2,0,3,4,1:T(8,128)(2,1)S(1)} all-reduce(f32[8,2,32,2,4]{2,0,3,4,1:T(8,128)S(1)} %copy.19), channel_id=1, replica_groups=mesh['blk'=8,'lblk'=4] {'lblk'}, use_global_device_ids=true, to_apply=%region_0.1 | all-reduce | flops 4096 | bytes 24576 | tf_op jit(solution)/shard_map/psum | solution.py:95
  52.7 0.2 convolution_bitcast_fusion
  52.9 0.9 %copy.20 = f32[8,2,4,1024]{3,2,1,0:T(4,128)} copy(f32[8,2,4,1024]{3,0,1,2:T(8,128)S(1)} %fusion.12) | data formatting | bytes 524288 | tf_op jit(solution)/shard_map/jit(_where)/select_n | solution.py:45
  (24 shorter events, 1.0 us)
Async XLA Ops:
  0.0 0.7 %copy-start.1 = (s32[2,4]{1,0:T(2,128)S(1)}, s32[2,4]{1,0:T(2,128)}, u32[]{:S(2)}) copy-start(s32[2,4]{1,0:T(2,128)} %param.7) | copy-start | bytes 100
  0.0 0.7 %copy-start.2 = (s32[2,4]{1,0:T(2,128)S(1)}, s32[2,4]{1,0:T(2,128)}, u32[]{:S(2)}) copy-start(s32[2,4]{1,0:T(2,128)} %param.6) | copy-start | bytes 100
  2.8 11.2 %collective-permute-start.1 = (bf16[8,2,1,4096]{3,2,1,0:T(2,128)(2,1)S(1)}, bf16[8,2,1,4096]{3,2,1,0:T(2,128)(2,1)S(1)}, u32[]{:S(2)}, u32[]{:S(2)}) collective-permute-start(bf16[8,2,1,4096]{3,2,1,0:T(2,128)(2,1)S(1)} %get-tuple-element.5), channel_id=1, source_target_pairs={{4,0},{8,4},{12,8},{16,12},{20,16},{24,20},{28,24},{5,1},{9,5},{13... | collective-permute-start | bytes 393224 | tf_op jit(solution)/shard_map/ppermute | solution.py:22
  4.1 15.7 %collective-permute-start = (bf16[8,2,1,4096]{3,2,1,0:T(2,128)(2,1)S(1)}, bf16[8,2,1,4096]{3,2,1,0:T(2,128)(2,1)S(1)}, u32[]{:S(2)}, u32[]{:S(2)}) collective-permute-start(bf16[8,2,1,4096]{3,2,1,0:T(2,128)(2,1)S(1)} %get-tuple-element.6), channel_id=1, source_target_pairs={{0,4},{4,8},{8,12},{12,16},{16,20},{20,24},{24,28},{1,5},{5,9},{9,... | collective-permute-start | bytes 393224 | tf_op jit(solution)/shard_map/ppermute | solution.py:21
  9.7 4.7 %collective-permute-start.2 = (bf16[8,2,4,1]{3,2,1,0:T(4,128)(2,1)S(1)}, bf16[8,2,4,1]{3,2,1,0:T(4,128)(2,1)S(1)}, u32[]{:S(2)}, u32[]{:S(2)}) collective-permute-start(bf16[8,2,4,1]{3,2,1,0:T(4,128)(2,1)S(1)} %get-tuple-element.7), channel_id=1, source_target_pairs={{0,1},{1,2},{2,3},{3,0},{4,5},{5,6},{6,7},{7,4},{8,9},{9,10},{10,1... | collective-permute-start | bytes 392 | tf_op jit(solution)/shard_map/ppermute | solution.py:21
  9.8 1.7 %copy-start.3 = (s32[32]{0:T(128)S(1)}, s32[32]{0:T(128)}, u32[]{:S(2)}) copy-start(s32[32]{0:T(128)} %param.8) | copy-start | bytes 388
  9.8 4.6 %collective-permute-start.3 = (bf16[8,2,4,1]{3,2,1,0:T(4,128)(2,1)S(1)}, bf16[8,2,4,1]{3,2,1,0:T(4,128)(2,1)S(1)}, u32[]{:S(2)}, u32[]{:S(2)}) collective-permute-start(bf16[8,2,4,1]{3,2,1,0:T(4,128)(2,1)S(1)} %get-tuple-element.8), channel_id=1, source_target_pairs={{1,0},{2,1},{3,2},{0,3},{5,4},{6,5},{7,6},{4,7},{9,8},{10,9},{11,1... | collective-permute-start | bytes 392 | tf_op jit(solution)/shard_map/ppermute | solution.py:22
  26.6 7.0 %copy-start = (bf16[4,8,4,1024]{3,2,1,0:T(4,128)(2,1)S(1)}, bf16[4,8,4,1024]{3,2,1,0:T(4,128)(2,1)}, u32[]{:S(2)}) copy-start(bf16[4,8,4,1024]{3,2,1,0:T(4,128)(2,1)} %param.9) | copy-start | bytes 786436
  27.7 12.4 %all-to-all-start = ((f32[8,1,512]{2,1,0:T(1,128)}), f32[8,1,512]{2,1,0:T(1,128)S(1)}, u32[]{:S(2)}, u32[]{:S(2)}) async-start(f32[8,1,512]{2,1,0:T(1,128)} %reshape.175), calls=%async_computation | async-start | bytes 32768 | tf_op jit(solution)/shard_map/all_to_all | solution.py:94
where the time goes:
time: 54.1 us; the launch traced here: 53.8 us
  starting transfers between devices  14.4 us (27%)
  waiting for transfers between devices  13.7 us (25%)
  blocking collectives  10.7 us (20%)
  other arithmetic  5.17 us (10%)
  local copies, waits for them, and re-layouts  4.95 us (9%)
  matrix products  4.74 us (9%)
    psum x1, blocking collectives, local(): summed = lax.psum(spread, 'lblk')  10.7 us
    all_to_all x1, waiting for transfers between devices, local(): lax.all_to_all(partial_value, 'blk', split_axis=4, concat_axis=2, tiled=T...  6.4 us
    all_to_all x1, starting transfers between devices, local(): lax.all_to_all(partial_value, 'blk', split_axis=4, concat_axis=2, tiled=T...  5.78 us
    ppermute x2, starting transfers between devices, padded(): before = lax.ppermute(last, axis, up)  5.6 us
    ppermute x2, waiting for transfers between devices, padded(): before = lax.ppermute(last, axis, up)  5.33 us
    ppermute x2, starting transfers between devices, padded(): after = lax.ppermute(initial, axis, down)  3.01 us
    dot_general x1, matrix products, local(): jnp.dot(flat_rows, sin_table, preferred_element_type=jnp.float32)  2.29 us
    convert_element_type x1, other arithmetic, local(): smooth = (centre + DIFFUSION * total).astype(jnp.bfloat16)  2.27 us
  transfers between devices with their start and end apart: 5, of which 3 were waited for; matrix products, arithmetic and copies ran while one was open for 2% of the time, Pallas kernels for 0%

commit v1 on v0

v1 whole, which is shorter than its diff:
```python
import math

import jax
import jax.numpy as jnp
from jax import lax
from jax.experimental import pallas as pl
from jax.experimental.pallas import tpu as pltpu
from jax.sharding import PartitionSpec as P

DIFFUSION = 0.2
LANES = 128

COS_TERMS = (1.0, -1.0 / 2, 1.0 / 24, -1.0 / 720, 1.0 / 40320, -1.0 / 3628800)
SIN_TERMS = (1.0, -1.0 / 6, 1.0 / 120, -1.0 / 5040, 1.0 / 362880)


def horner(terms, square):
    total = jnp.full_like(square, terms[-1])
    for term in terms[-2::-1]:
        total = total * square + term
    return total


def circle(index, turn):
    index = index & (turn - 1)
    quadrant = (index * 4 + turn // 2) >> (turn.bit_length() - 1)
    rest = (index - quadrant * (turn // 4)).astype(jnp.float32) * (2.0 * math.pi / turn)
    square = rest * rest
    cosine = horner(COS_TERMS, square)
    sine = rest * horner(SIN_TERMS, square)
    odd = (quadrant & 1) == 1
    swapped_cos = jnp.where(odd, sine, cosine)
    swapped_sin = jnp.where(odd, cosine, sine)
    cos_sign = ((quadrant + 1) & 2) == 2
    sin_sign = (quadrant & 2) == 2
    return (
        jnp.where(cos_sign, -swapped_cos, swapped_cos),
        jnp.where(sin_sign, -swapped_sin, swapped_sin),
    )


def iota(shape, axis):
    return lax.broadcasted_iota(jnp.int32, shape, axis)


def fourier_kernel(maps, band, quarter, ring, owned, copies, chunk, chunks):
    pieces = quarter // LANES
    rows = 2 * pieces * band

    def body(sky_hbm, start_hbm, count_hbm, modes_hbm, flat_hbm, out_ref, aux_ref, sky_ref, start_ref, count_ref, modes_ref, flat_ref, sems, sky_sems):
        small = [
            pltpu.make_async_copy(modes_hbm, modes_ref, sems.at[0]),
            pltpu.make_async_copy(flat_hbm, flat_ref, sems.at[1]),
            pltpu.make_async_copy(start_hbm, start_ref, sems.at[2]),
            pltpu.make_async_copy(count_hbm, count_ref, sems.at[3]),
        ]
        for copy in small:
            copy.start()
        sky_copies = [
            pltpu.make_async_copy(
                sky_hbm.at[pl.ds(x * rows, rows)], sky_ref.at[pl.ds(x * rows, rows)], sky_sems.at[x]
            )
            for x in range(maps)
        ]
        for copy in sky_copies:
            copy.start()
        first_pixel = lax.axis_index("lblk") * quarter
        block = lax.axis_index("blk")
        for copy in small:
            copy.wait()

        row = iota((8, LANES), 0) % owned
        lane = iota((8, LANES), 1)
        mine = jnp.zeros((8, LANES), jnp.int32)
        for s in range(owned):
            mine = jnp.where(row == s, flat_ref[block * owned + s], mine)
        scale = DIFFUSION / math.sqrt(ring)
        step_cos, _ = circle(mine, ring)
        turn_cos, turn_sin = circle(mine * (lane % band % 2), 2 * ring)
        aux_ref[0] = scale * (1.0 + 2.0 * step_cos)
        aux_ref[1] = turn_cos
        aux_ref[2] = jnp.where(lane < LANES // 2, turn_sin, -turn_sin)
        aux_ref[3] = mine.astype(jnp.float32)

        masks = []
        row8 = iota((8, LANES), 0)
        lane8 = iota((8, LANES), 1)
        for h in range(2):
            start = jnp.zeros((8, LANES), jnp.int32)
            count = jnp.zeros((8, LANES), jnp.int32)
            for k in range(band):
                start = jnp.where(row8 % band == k, start_ref[h, k], start)
                count = jnp.where(row8 % band == k, count_ref[h, k], count)
            shifted = first_pixel + (row8 // band) * LANES + lane8 - start
            for t in range(pieces * band // 8):
                offset = (shifted + t * (8 // band) * LANES) & (ring - 1)
                masks.append(jnp.where(offset < count, 1.0, 0.0))
        mask = jnp.concatenate(masks, axis=0).astype(jnp.bfloat16)

        def tables(modes):
            lane_modes = jnp.concatenate([modes] * 4, axis=1)
            width = 4 * chunk
            kind = iota((1, width), 1) // chunk
            cosine, sine = circle(iota((LANES, width), 0) * lane_modes, ring)
            table = jnp.where(kind % 2 == 0, cosine, sine)
            high = table.astype(jnp.bfloat16)
            low = (table - high.astype(jnp.float32)).astype(jnp.bfloat16)
            pixel = first_pixel + (iota((pieces * band, width), 0) // band) * LANES
            cosine, sine = circle(pixel * lane_modes, ring)
            turn = jnp.where(kind == 0, cosine, jnp.where(kind == 3, -cosine, -sine))
            return jnp.concatenate([high, low], axis=0), turn

        def sums(values, table, turn):
            wide = jnp.concatenate([values, values], axis=1)
            product = jnp.dot(wide, table, preferred_element_type=jnp.float32)
            parts = []
            for h in range(2):
                total = None
                for t in range(pieces * band // 8):
                    at = h * pieces * band + t * 8
                    term = product[at : at + 8] * turn[t * 8 : t * 8 + 8]
                    total = term if total is None else total + term
                folded = total[:band]
                for k in range(band, 8, band):
                    folded = folded + total[k : k + band]
                parts.append(folded)
            return jnp.concatenate(parts, axis=0)

        def send(gathered, owners, index):
            turned = gathered.T
            real = turned[:chunk] + turned[chunk : 2 * chunk]
            imag = turned[2 * chunk : 3 * chunk] + turned[3 * chunk :]
            both = jnp.concatenate([real, imag], axis=1)
            for o in range(owners):
                for c in range(copies):
                    out_ref[index * owners * copies + o * copies + c] = both[o * owned : (o + 1) * owned]

        owners = chunk // owned
        if chunks == 1:
            table, turn = tables(modes_ref[0])
            found = []
            for x in range(maps):
                sky_copies[x].wait()
                found.append(sums(sky_ref[pl.ds(x * rows, rows)] * mask, table, turn))
            send(jnp.concatenate(found, axis=0), owners, 0)
        else:
            for x in range(maps):
                sky_copies[x].wait()
                sky_ref[pl.ds(x * rows, rows)] = sky_ref[pl.ds(x * rows, rows)] * mask

            def step(index, carry):
                table, turn = tables(modes_ref[index])
                found = [sums(sky_ref[pl.ds(x * rows, rows)], table, turn) for x in range(maps)]
                send(jnp.concatenate(found, axis=0), owners, index)
                return carry

            lax.fori_loop(0, chunks, step, 0)

    return body


def legendre_kernel(maps, band, owned, blocks, copies, degrees, ring):
    scale = DIFFUSION / math.sqrt(ring)
    cycles = blocks * band

    def body(sums_ref, aux_ref, legendre_ref, out_ref):
        lane = iota((1, LANES), 1)
        cycle = lane % band
        south = (lane // band) % 2 == 1
        parts = []
        for b in range(blocks):
            total = sums_ref[b * copies]
            for c in range(1, copies):
                total = total + sums_ref[b * copies + c]
            parts.append(total)
        here = jnp.concatenate(parts, axis=0)
        rows = blocks * owned
        none = jnp.zeros((owned, LANES), jnp.float32)
        prior = jnp.concatenate([none, here[:-owned]], axis=0)
        later = jnp.concatenate([here[owned:], none], axis=0)

        def moved(value, shift):
            return pltpu.roll(value, shift % LANES, 1)

        above = jnp.where(cycle == 0, moved(prior, 1 - band), moved(here, 1))
        other = jnp.where(south, moved(here, band), moved(here, -band))
        is_last = iota((rows, 1), 0) >= rows - owned
        edge = jnp.where(is_last, other, moved(later, band - 1))
        below = jnp.where(cycle == band - 1, edge, moved(here, -1))

        def wide(value):
            return jnp.concatenate([value] * (rows // 8), axis=0)

        smooth = wide(aux_ref[0]) * here + scale * (above + below)
        turned = smooth * wide(aux_ref[1]) + moved(smooth, LANES // 2) * wide(aux_ref[2])
        folded = jnp.where(south, moved(turned, band) - turned, turned + moved(turned, -band))
        folded = folded.astype(jnp.bfloat16)

        depth = owned * cycles
        row = iota((rows, depth), 0)
        column = iota((rows, depth), 1)
        spread = (row // owned == (column // band) % blocks) & (row % owned == column // cycles)
        spread = jnp.where(spread, 1.0, 0.0).astype(jnp.bfloat16)
        across = lax.dot_general(
            folded, spread, (((0,), (0,)), ((), ())), preferred_element_type=jnp.float32
        )
        match = iota((LANES, depth), 0) % band == iota((LANES, depth), 1) % band
        across = jnp.where(match, across, 0.0).astype(jnp.bfloat16)
        height = 2 * maps * 2 * owned
        row = iota((height, LANES), 0)
        column = iota((height, LANES), 1)
        fold, x, part = row // (maps * 2 * owned), (row // (2 * owned)) % maps, (row // owned) % 2
        pick = column // band == part * (maps * 2) + x * 2 + fold
        pick = jnp.where(pick, 1.0, 0.0).astype(jnp.bfloat16)
        weights = jnp.dot(pick, across, preferred_element_type=jnp.float32)
        match = iota((height, depth), 0) % owned == iota((height, depth), 1) // cycles
        weights = jnp.where(match, weights, 0.0).astype(jnp.bfloat16)

        sums = jnp.dot(weights, legendre_ref[...], preferred_element_type=jnp.float32)
        mode = aux_ref[3].astype(jnp.int32)
        half = height // 2
        group = 8 // owned
        columns = degrees // LANES
        first = lax.axis_index("lblk") * degrees
        picked = []
        for j in range(columns):
            degree = first + j * LANES + iota((8, LANES), 1)
            even = ((degree + mode) & 1) == 0
            inside = degree >= mode
            line = []
            for i in range(half // 8):
                plus = sums[i * 8 : i * 8 + 8, j * LANES : (j + 1) * LANES]
                minus = sums[half + i * 8 : half + i * 8 + 8, j * LANES : (j + 1) * LANES]
                line.append(jnp.where(inside, jnp.where(even, plus, minus), 0.0))
            picked.append(line)
        for i in range(half // 8):
            for g in range(group):
                for j in range(columns):
                    at = ((i * group + g) * columns + j) * owned
                    out_ref[at : at + owned] = picked[j][i][g * owned : (g + 1) * owned]

    return body


def local(sky, arc_start, arc_count, owner_modes, legendre):
    maps, _, band, quarter = sky.shape
    slots = owner_modes.shape[0]
    owned, groups, _, degrees = legendre.shape
    blocks, copies = lax.axis_size("blk"), lax.axis_size("lblk")
    ring = quarter * copies
    chunk = min(slots, LANES // 4)
    chunks = slots // chunk
    pieces = quarter // LANES
    sky_rows = sky.reshape(maps, 2, band, pieces, LANES).transpose(0, 1, 3, 2, 4)
    sky_rows = sky_rows.reshape(maps * 2 * pieces * band, LANES)
    anywhere = pl.BlockSpec(memory_space=pl.ANY)
    whole = pl.BlockSpec(memory_space=pltpu.VMEM)
    partial, aux = pl.pallas_call(
        fourier_kernel(maps, band, quarter, ring, owned, copies, chunk, chunks),
        out_shape=(
            jax.ShapeDtypeStruct((blocks * copies, owned, LANES), jnp.float32),
            jax.ShapeDtypeStruct((4, 8, LANES), jnp.float32),
        ),
        in_specs=[anywhere] * 5,
        out_specs=(whole, whole),
        scratch_shapes=[
            pltpu.VMEM(sky_rows.shape, jnp.bfloat16),
            pltpu.SMEM(arc_start.shape, jnp.int32),
            pltpu.SMEM(arc_count.shape, jnp.int32),
            pltpu.VMEM((chunks, 1, chunk), jnp.int32),
            pltpu.SMEM((slots,), jnp.int32),
            pltpu.SemaphoreType.DMA((4,)),
            pltpu.SemaphoreType.DMA((maps,)),
        ],
        name="fourier",
    )(sky_rows, arc_start, arc_count, owner_modes.reshape(chunks, 1, chunk), owner_modes)
    received = lax.all_to_all(partial, ("blk", "lblk"), split_axis=0, concat_axis=0, tiled=True)
    columns = degrees // LANES
    result = pl.pallas_call(
        legendre_kernel(maps, band, owned, blocks, copies, degrees, ring),
        out_shape=jax.ShapeDtypeStruct((maps * 2 * columns * owned, LANES), jnp.float32),
        in_specs=[whole] * 3,
        out_specs=whole,
        name="legendre",
    )(received, aux, legendre.reshape(owned * groups * band, degrees))
    result = result.reshape(maps, 2, columns, owned, LANES).transpose(0, 1, 3, 2, 4)
    return result.reshape(maps, 2, owned, degrees)


def solution(mesh):
    return jax.shard_map(
        local,
        mesh=mesh,
        in_specs=(
            P(None, None, "blk", "lblk"),
            P(None, "blk"),
            P(None, "blk"),
            P(),
            P("blk", None, None, "lblk"),
        ),
        out_specs=P(None, None, "blk", "lblk"),
        check_vma=False,
    )
```

time: 54.1 us -> 21.7 us (0.40)
  blocking collectives: 10.7 us -> 0 us
  starting transfers between devices: 14.4 us -> 7.33 us
  waiting for transfers between devices: 13.7 us -> 6.64 us
  Pallas kernels: 0 us -> 6.13 us
  other arithmetic: 5.17 us -> 0 us
  matrix products: 4.74 us -> 0 us
  local copies, waits for them, and re-layouts: 4.95 us -> 1.37 us
    psum x1 -> x0, blocking collectives: 10.7 us -> none  [local(): summed = lax.psum(spread, 'lblk')]
    ppermute x4 -> x0, starting transfers between devices: 8.61 us -> none  [the longest x2 5.6 us: padded(): before = lax.ppermute(last, axis, up)]
    ppermute x4 -> x0, waiting for transfers between devices: 7.29 us -> none  [the longest x2 5.33 us: padded(): before = lax.ppermute(last, axis, up)]
    pallas_call x0 -> x2, Pallas kernels: none -> 6.13 us  [the longest x1 3.68 us: local(): pl.pallas_call(fourier_kernel(maps, band, quarter, ring, owned, copies, c...]
    dot_general x3 -> x0, matrix products: 4.74 us -> none  [the longest x1 2.29 us: local(): jnp.dot(flat_rows, sin_table, preferred_element_type=jnp.float32)]
    convert_element_type x1 -> x0, other arithmetic: 2.27 us -> none  [local(): smooth = (centre + DIFFUSION * total).astype(jnp.bfloat16)]
    select_n x4 -> x0, other arithmetic: 1.77 us -> none  [the longest x1 1.3 us: local(): masked = jnp.where(kept_mask[None], sky, jnp.zeros((), jnp.bfloat16))]
    all_to_all x1, starting transfers between devices: 5.78 us -> 7.33 us  [local(): lax.all_to_all(partial, ('blk', 'lblk'), split_axis=0, concat_axis=0, til...]
  transfers between devices with their start and end apart: 5 -> 1, of which waited for: 3 -> 1; matrix products, arithmetic and copies ran while one was open for 2% -> 4% of each run, Pallas kernels for 0% -> 0%
where the time goes in v1:
time: 21.7 us; the launch traced here: 21.5 us
  starting transfers between devices  7.33 us (34%)
  waiting for transfers between devices  6.64 us (31%)
  Pallas kernels  6.13 us (28%)
  local copies, waits for them, and re-layouts  1.37 us (6%)
    all_to_all x1, starting transfers between devices, local(): lax.all_to_all(partial, ('blk', 'lblk'), split_axis=0, concat_axis=0, til...  7.33 us
    all_to_all x1, waiting for transfers between devices, local(): lax.all_to_all(partial, ('blk', 'lblk'), split_axis=0, concat_axis=0, til...  6.64 us
    pallas_call x1, Pallas kernels, local(): pl.pallas_call(fourier_kernel(maps, band, quarter, ring, owned, copies, c...  3.68 us
    pallas_call x1, Pallas kernels, local(): pl.pallas_call(legendre_kernel(maps, band, owned, blocks, copies, degrees...  2.45 us
    reshape x1, local copies, waits for them, and re-layouts, local(): legendre.reshape(owned * groups * band, degrees)  0.76 us
    unnamed x4, local copies, waits for them, and re-layouts  0.62 us
  transfers between devices with their start and end apart: 1, of which 1 were waited for; matrix products, arithmetic and copies ran while one was open for 4% of the time, Pallas kernels for 0%

profile of v1, /device:TPU:0, one launch (start us, length us, event | category | flops | bytes accessed | tf_op | source)
XLA Modules:
  0.0 21.5 jit_solution(3316518492976039363)
XLA Ops:
  0.0 0.0 copy-start.1
  0.0 3.7 %fourier.1 = (f32[32,4,128]{2,1,0:T(4,128)}, f32[4,8,128]{2,1,0:T(8,128)}) custom-call(bf16[2048,128]{1,0:T(8,128)(2,1)} %bitcast.11, s32[2,4]{1,0:T(2,128)} %start_hbm.1, s32[2,4]{1,0:T(2,128)} %count_hbm.1, s32[1,1,32]{2,1,0:T(1,128)} %bitcast.12, s32[32]{0:T(128)} %flat_hbm.1), custom_call_target="tpu_custom_call" | custom-call | tf_op jit(solution)/shard_map/fourier/pallas_call | solution.py:258
  3.7 7.3 %all-to-all-start = ((f32[32,4,128]{2,1,0:T(4,128)}), f32[32,4,128]{2,1,0:T(4,128)S(1)}, u32[]{:S(2)}, u32[]{:S(2)}) async-start(f32[32,4,128]{2,1,0:T(4,128)} %get-tuple-element.7), calls=%async_computation | async-start | bytes 131072 | tf_op jit(solution)/shard_map/all_to_all | solution.py:277
  11.0 0.0 copy-done.1
  11.0 0.8 %reshape.21.legendre_ref = bf16[128,1024]{1,0:T(8,128)(2,1)} reshape(bf16[4,8,4,1024]{3,2,1,0:T(4,128)(2,1)S(1)} %copy-done.1) | data formatting | bytes 524288 | tf_op jit(solution)/shard_map/reshape | solution.py:285
  11.8 6.6 %all-to-all-done.sums_ref = f32[32,4,128]{2,1,0:T(4,128)S(1)} async-done(((f32[32,4,128]{2,1,0:T(4,128)}), f32[32,4,128]{2,1,0:T(4,128)S(1)}, u32[]{:S(2)}, u32[]{:S(2)}) %all-to-all-start) | async-done | bytes 65568 | tf_op jit(solution)/shard_map/all_to_all | solution.py:277
  18.4 0.0 copy-start
  18.4 0.6 %copy-done = f32[32,4,128]{2,1,0:T(4,128)} copy-done((f32[32,4,128]{2,1,0:T(4,128)}, f32[32,4,128]{2,1,0:T(4,128)S(1)}, u32[]{:S(2)}) %copy-start) | copy-done | bytes 65560
  19.0 2.5 %legendre.1 = f32[512,128]{1,0:T(8,128)} custom-call(f32[32,4,128]{2,1,0:T(4,128)} %copy-done, f32[4,8,128]{2,1,0:T(8,128)} %get-tuple-element.8.aux_ref, bf16[128,1024]{1,0:T(8,128)(2,1)} %reshape.21.legendre_ref), custom_call_target="tpu_custom_call" | custom-call | tf_op jit(solution)/shard_map/legendre/pallas_call | solution.py:279
Async XLA Ops:
  0.0 11.0 %copy-start.1 = (bf16[4,8,4,1024]{3,2,1,0:T(4,128)(2,1)S(1)}, bf16[4,8,4,1024]{3,2,1,0:T(4,128)(2,1)}, u32[]{:S(2)}) copy-start(bf16[4,8,4,1024]{3,2,1,0:T(4,128)(2,1)} %param.9) | copy-start | bytes 786436
  3.7 14.7 %all-to-all-start = ((f32[32,4,128]{2,1,0:T(4,128)}), f32[32,4,128]{2,1,0:T(4,128)S(1)}, u32[]{:S(2)}, u32[]{:S(2)}) async-start(f32[32,4,128]{2,1,0:T(4,128)} %get-tuple-element.7), calls=%async_computation | async-start | bytes 131072 | tf_op jit(solution)/shard_map/all_to_all | solution.py:277
  18.4 0.6 %copy-start = (f32[32,4,128]{2,1,0:T(4,128)}, f32[32,4,128]{2,1,0:T(4,128)S(1)}, u32[]{:S(2)}) copy-start(f32[32,4,128]{2,1,0:T(4,128)S(1)} %all-to-all-done.sums_ref) | copy-start | bytes 196612

commit v2 on v1

--- a/solution.py
+++ b/solution.py
@@ -9,6 +9,8 @@
 
 DIFFUSION = 0.2
 LANES = 128
+STEP = 4
+ROOM = pltpu.CompilerParams(vmem_limit_bytes=28 * 2**20)
 
 COS_TERMS = (1.0, -1.0 / 2, 1.0 / 24, -1.0 / 720, 1.0 / 40320, -1.0 / 3628800)
 SIN_TERMS = (1.0, -1.0 / 6, 1.0 / 120, -1.0 / 5040, 1.0 / 362880)
@@ -43,118 +45,90 @@
     return lax.broadcasted_iota(jnp.int32, shape, axis)
 
 
-def fourier_kernel(maps, band, quarter, ring, owned, copies, chunk, chunks):
+def table_kernel(band, quarter, ring, owned, chunk):
     pieces = quarter // LANES
-    rows = 2 * pieces * band
-
-    def body(sky_hbm, start_hbm, count_hbm, modes_hbm, flat_hbm, out_ref, aux_ref, sky_ref, start_ref, count_ref, modes_ref, flat_ref, sems, sky_sems):
-        small = [
-            pltpu.make_async_copy(modes_hbm, modes_ref, sems.at[0]),
-            pltpu.make_async_copy(flat_hbm, flat_ref, sems.at[1]),
-            pltpu.make_async_copy(start_hbm, start_ref, sems.at[2]),
-            pltpu.make_async_copy(count_hbm, count_ref, sems.at[3]),
-        ]
-        for copy in small:
-            copy.start()
-        sky_copies = [
-            pltpu.make_async_copy(
-                sky_hbm.at[pl.ds(x * rows, rows)], sky_ref.at[pl.ds(x * rows, rows)], sky_sems.at[x]
-            )
-            for x in range(maps)
-        ]
-        for copy in sky_copies:
-            copy.start()
+    width = 4 * chunk
+
+    def body(start_ref, count_ref, modes_ref, mask_ref, table_ref, turn_ref, aux_ref):
         first_pixel = lax.axis_index("lblk") * quarter
         block = lax.axis_index("blk")
-        for copy in small:
-            copy.wait()
-
-        row = iota((8, LANES), 0) % owned
+        row = iota((8, LANES), 0)
         lane = iota((8, LANES), 1)
         mine = jnp.zeros((8, LANES), jnp.int32)
         for s in range(owned):
-            mine = jnp.where(row == s, flat_ref[block * owned + s], mine)
-        scale = DIFFUSION / math.sqrt(ring)
+            mine = jnp.where(row % owned == s, modes_ref[block * owned + s], mine)
         step_cos, _ = circle(mine, ring)
         turn_cos, turn_sin = circle(mine * (lane % band % 2), 2 * ring)
-        aux_ref[0] = scale * (1.0 + 2.0 * step_cos)
+        aux_ref[0] = DIFFUSION / math.sqrt(ring) * (1.0 + 2.0 * step_cos)
         aux_ref[1] = turn_cos
         aux_ref[2] = jnp.where(lane < LANES // 2, turn_sin, -turn_sin)
         aux_ref[3] = mine.astype(jnp.float32)
 
         masks = []
-        row8 = iota((8, LANES), 0)
-        lane8 = iota((8, LANES), 1)
         for h in range(2):
             start = jnp.zeros((8, LANES), jnp.int32)
             count = jnp.zeros((8, LANES), jnp.int32)
             for k in range(band):
-                start = jnp.where(row8 % band == k, start_ref[h, k], start)
-                count = jnp.where(row8 % band == k, count_ref[h, k], count)
-            shifted = first_pixel + (row8 // band) * LANES + lane8 - start
+                start = jnp.where(row % band == k, start_ref[h, k], start)
+                count = jnp.where(row % band == k, count_ref[h, k], count)
+            shifted = first_pixel + (row // band) * LANES + lane - start
             for t in range(pieces * band // 8):
                 offset = (shifted + t * (8 // band) * LANES) & (ring - 1)
                 masks.append(jnp.where(offset < count, 1.0, 0.0))
-        mask = jnp.concatenate(masks, axis=0).astype(jnp.bfloat16)
-
-        def tables(modes):
-            lane_modes = jnp.concatenate([modes] * 4, axis=1)
-            width = 4 * chunk
-            kind = iota((1, width), 1) // chunk
-            cosine, sine = circle(iota((LANES, width), 0) * lane_modes, ring)
+        mask_ref[...] = jnp.concatenate(masks, axis=0).astype(jnp.bfloat16)
+
+        kind = iota((1, width), 1) // chunk
+        column = iota((1, width), 1) % chunk
+        for g in range(modes_ref.shape[0] // chunk):
+            modes = jnp.zeros((1, width), jnp.int32)
+            for s in range(chunk):
+                modes = jnp.where(column == s, modes_ref[g * chunk + s], modes)
+            cosine, sine = circle(iota((LANES, width), 0) * modes, ring)
             table = jnp.where(kind % 2 == 0, cosine, sine)
             high = table.astype(jnp.bfloat16)
-            low = (table - high.astype(jnp.float32)).astype(jnp.bfloat16)
+            table_ref[g, :LANES] = high
+            table_ref[g, LANES:] = (table - high.astype(jnp.float32)).astype(jnp.bfloat16)
             pixel = first_pixel + (iota((pieces * band, width), 0) // band) * LANES
-            cosine, sine = circle(pixel * lane_modes, ring)
-            turn = jnp.where(kind == 0, cosine, jnp.where(kind == 3, -cosine, -sine))
-            return jnp.concatenate([high, low], axis=0), turn
-
-        def sums(values, table, turn):
-            wide = jnp.concatenate([values, values], axis=1)
-            product = jnp.dot(wide, table, preferred_element_type=jnp.float32)
-            parts = []
-            for h in range(2):
-                total = None
-                for t in range(pieces * band // 8):
-                    at = h * pieces * band + t * 8
-                    term = product[at : at + 8] * turn[t * 8 : t * 8 + 8]
-                    total = term if total is None else total + term
-                folded = total[:band]
-                for k in range(band, 8, band):
-                    folded = folded + total[k : k + band]
-                parts.append(folded)
-            return jnp.concatenate(parts, axis=0)
-
-        def send(gathered, owners, index):
-            turned = gathered.T
+            cosine, sine = circle(pixel * modes, ring)
+            turn_ref[g] = jnp.where(kind == 0, cosine, jnp.where(kind == 3, -cosine, -sine))
+
+    return body
+
+
+def fourier_kernel(maps, band, pieces, owned, copies, chunk, chunks, step):
+    rows = 2 * pieces * band
+    owners = chunk // owned
+
+    def body(sky_ref, mask_ref, table_ref, turn_ref, out_ref):
+        def run(g):
+            found = []
+            for x in range(0, maps, step):
+                values = [sky_ref[(x + i) * rows : (x + i + 1) * rows] * mask_ref[...] for i in range(step)]
+                values = jnp.concatenate(values, axis=0)
+                wide = jnp.concatenate([values, values], axis=1)
+                product = jnp.dot(wide, table_ref[g], preferred_element_type=jnp.float32)
+                for h in range(2 * step):
+                    total = None
+                    for t in range(pieces * band // 8):
+                        at = h * pieces * band + t * 8
+                        term = product[at : at + 8] * turn_ref[g, t * 8 : t * 8 + 8]
+                        total = term if total is None else total + term
+                    folded = total[:band]
+                    for k in range(band, 8, band):
+                        folded = folded + total[k : k + band]
+                    found.append(folded)
+            turned = jnp.concatenate(found, axis=0).T
             real = turned[:chunk] + turned[chunk : 2 * chunk]
             imag = turned[2 * chunk : 3 * chunk] + turned[3 * chunk :]
             both = jnp.concatenate([real, imag], axis=1)
             for o in range(owners):
                 for c in range(copies):
-                    out_ref[index * owners * copies + o * copies + c] = both[o * owned : (o + 1) * owned]
-
-        owners = chunk // owned
+                    out_ref[(g * owners + o) * copies + c] = both[o * owned : (o + 1) * owned]
+
         if chunks == 1:
-            table, turn = tables(modes_ref[0])
-            found = []
-            for x in range(maps):
-                sky_copies[x].wait()
-                found.append(sums(sky_ref[pl.ds(x * rows, rows)] * mask, table, turn))
-            send(jnp.concatenate(found, axis=0), owners, 0)
+            run(0)
         else:
-            for x in range(maps):
-                sky_copies[x].wait()
-                sky_ref[pl.ds(x * rows, rows)] = sky_ref[pl.ds(x * rows, rows)] * mask
-
-            def step(index, carry):
-                table, turn = tables(modes_ref[index])
-                found = [sums(sky_ref[pl.ds(x * rows, rows)], table, turn) for x in range(maps)]
-                send(jnp.concatenate(found, axis=0), owners, index)
-                return carry
-
-            lax.fori_loop(0, chunks, step, 0)
+            lax.fori_loop(0, chunks, lambda g, _: run(g), None)
 
     return body
 
@@ -242,6 +216,10 @@
     return body
 
 
+def on_chip(value):
+    return pltpu.with_memory_space_constraint(value, pltpu.VMEM)
+
+
 def local(sky, arc_start, arc_count, owner_modes, legendre):
     maps, _, band, quarter = sky.shape
     slots = owner_modes.shape[0]
@@ -253,27 +231,30 @@
     pieces = quarter // LANES
     sky_rows = sky.reshape(maps, 2, band, pieces, LANES).transpose(0, 1, 3, 2, 4)
     sky_rows = sky_rows.reshape(maps * 2 * pieces * band, LANES)
-    anywhere = pl.BlockSpec(memory_space=pl.ANY)
+    scalars = pl.BlockSpec(memory_space=pltpu.SMEM)
     whole = pl.BlockSpec(memory_space=pltpu.VMEM)
-    partial, aux = pl.pallas_call(
-        fourier_kernel(maps, band, quarter, ring, owned, copies, chunk, chunks),
+    mask, table, turn, aux = pl.pallas_call(
+        table_kernel(band, quarter, ring, owned, chunk),
         out_shape=(
-            jax.ShapeDtypeStruct((blocks * copies, owned, LANES), jnp.float32),
-            jax.ShapeDtypeStruct((4, 8, LANES), jnp.float32),
+            pltpu.VMEM((2 * pieces * band, LANES), jnp.bfloat16),
+            pltpu.VMEM((chunks, 2 * LANES, 4 * chunk), jnp.bfloat16),
+            pltpu.VMEM((chunks, pieces * band, 4 * chunk), jnp.float32),
+            pltpu.VMEM((4, 8, LANES), jnp.float32),
         ),
-        in_specs=[anywhere] * 5,
-        out_specs=(whole, whole),
-        scratch_shapes=[
-            pltpu.VMEM(sky_rows.shape, jnp.bfloat16),
-            pltpu.SMEM(arc_start.shape, jnp.int32),
-            pltpu.SMEM(arc_count.shape, jnp.int32),
-            pltpu.VMEM((chunks, 1, chunk), jnp.int32),
-            pltpu.SMEM((slots,), jnp.int32),
-            pltpu.SemaphoreType.DMA((4,)),
-            pltpu.SemaphoreType.DMA((maps,)),
-        ],
+        in_specs=[scalars] * 3,
+        out_specs=(whole,) * 4,
+        cost_estimate=pl.CostEstimate(flops=10**9, bytes_accessed=4 * 10**6, transcendentals=10**6),
+        compiler_params=ROOM,
+        name="tables",
+    )(arc_start, arc_count, owner_modes)
+    partial = pl.pallas_call(
+        fourier_kernel(maps, band, pieces, owned, copies, chunk, chunks, STEP),
+        out_shape=pltpu.VMEM((blocks * copies, owned, LANES), jnp.float32),
+        in_specs=[whole] * 4,
+        out_specs=whole,
+        compiler_params=ROOM,
         name="fourier",
-    )(sky_rows, arc_start, arc_count, owner_modes.reshape(chunks, 1, chunk), owner_modes)
+    )(*(on_chip(v) for v in (sky_rows, mask, table, turn)))
     received = lax.all_to_all(partial, ("blk", "lblk"), split_axis=0, concat_axis=0, tiled=True)
     columns = degrees // LANES
     result = pl.pallas_call(
@@ -281,8 +262,9 @@
         out_shape=jax.ShapeDtypeStruct((maps * 2 * columns * owned, LANES), jnp.float32),
         in_specs=[whole] * 3,
         out_specs=whole,
+        compiler_params=ROOM,
         name="legendre",
-    )(received, aux, legendre.reshape(owned * groups * band, degrees))
+    )(on_chip(received), on_chip(aux), on_chip(legendre.reshape(owned * groups * band, degrees)))
     result = result.reshape(maps, 2, columns, owned, LANES).transpose(0, 1, 3, 2, 4)
     return result.reshape(maps, 2, owned, degrees)
 

time: 21.7 us -> 20.6 us (0.949)
  Pallas kernels: 6.13 us -> 3.53 us
  local copies, waits for them, and re-layouts: 1.37 us -> 2.14 us
  waiting for transfers between devices: 6.64 us -> 7.33 us
    pallas_call x1 -> x2, Pallas kernels: 3.68 us -> 2.08 us  [the longest x1 1.24 us: local(): pl.pallas_call(fourier_kernel(maps, band, pieces, owned, copies, chunk, c...]
    unnamed x4 -> x10, local copies, waits for them, and re-layouts: 0.62 us -> 2.08 us
    pallas_call x1, Pallas kernels: 2.45 us -> 1.45 us  [local(): pl.pallas_call(legendre_kernel(maps, band, owned, blocks, copies, degrees...]
    reshape x1, local copies, waits for them, and re-layouts: 0.76 us -> 0.06 us  [local(): legendre.reshape(owned * groups * band, degrees)]
    all_to_all x1, waiting for transfers between devices: 6.64 us -> 7.33 us  [local(): lax.all_to_all(partial, ('blk', 'lblk'), split_axis=0, concat_axis=0, til...]
  transfers between devices with their start and end apart: 1 -> 1, of which waited for: 1 -> 1; matrix products, arithmetic and copies ran while one was open for 4% -> 0% of each run, Pallas kernels for 0% -> 0%
where the time goes in v2:
time: 20.6 us; the launch traced here: 20.4 us
  waiting for transfers between devices  7.33 us (36%)
  starting transfers between devices  7.32 us (36%)
  Pallas kernels  3.53 us (17%)
  local copies, waits for them, and re-layouts  2.14 us (10%)
    all_to_all x1, waiting for transfers between devices, local(): lax.all_to_all(partial, ('blk', 'lblk'), split_axis=0, concat_axis=0, til...  7.33 us
    all_to_all x1, starting transfers between devices, local(): lax.all_to_all(partial, ('blk', 'lblk'), split_axis=0, concat_axis=0, til...  7.32 us
    unnamed x10, local copies, waits for them, and re-layouts  2.08 us
    pallas_call x1, Pallas kernels, local(): pl.pallas_call(legendre_kernel(maps, band, owned, blocks, copies, degrees...  1.45 us
    pallas_call x1, Pallas kernels, local(): pl.pallas_call(fourier_kernel(maps, band, pieces, owned, copies, chunk, c...  1.24 us
    pallas_call x1, Pallas kernels, local(): pl.pallas_call(table_kernel(band, quarter, ring, owned, chunk), out_shape...  0.84 us
  transfers between devices with their start and end apart: 1, of which 1 were waited for; matrix products, arithmetic and copies ran while one was open for 0% of the time, Pallas kernels for 0%

profile of v2, /device:TPU:0, one launch (start us, length us, event | category | flops | bytes accessed | tf_op | source)
XLA Modules:
  0.0 20.4 jit_solution(11861159556193398898)
XLA Ops:
  0.0 0.0 copy-start
  0.0 0.0 copy-start.1
  0.0 0.7 %copy-done.1 = s32[2,4]{1,0:T(2,128)S(1)} copy-done((s32[2,4]{1,0:T(2,128)S(1)}, s32[2,4]{1,0:T(2,128)}, u32[]{:S(2)}) %copy-start.1) | copy-done | bytes 56
  0.7 0.0 copy-start.2
  0.7 0.7 %copy-done.2 = s32[2,4]{1,0:T(2,128)S(1)} copy-done((s32[2,4]{1,0:T(2,128)S(1)}, s32[2,4]{1,0:T(2,128)}, u32[]{:S(2)}) %copy-start.2) | copy-done | bytes 56
  1.4 0.0 copy-start.3
  1.4 0.7 %copy-done.3 = s32[32]{0:T(128)S(1)} copy-done((s32[32]{0:T(128)S(1)}, s32[32]{0:T(128)}, u32[]{:S(2)}) %copy-start.3) | copy-done | bytes 152
  2.1 0.8 %tables.1 = (bf16[256,128]{1,0:T(8,128)(2,1)S(1)}, bf16[1,256,128]{2,1,0:T(8,128)(2,1)S(1)}, f32[1,128,128]{2,1,0:T(8,128)S(1)}, f32[4,8,128]{2,1,0:T(8,128)S(1)}) custom-call(s32[2,4]{1,0:T(2,128)S(1)} %copy-done.1, s32[2,4]{1,0:T(2,128)S(1)} %copy-done.2, s32[32]{0:T(128)S(1)} %copy-done.3), custom_call_target="tpu_custom_call" | custom-call | flops 1000000000 | bytes 4000000 | tf_op jit(solution)/shard_map/tables/pallas_call | solution.py:236
  2.9 0.0 copy-done
  2.9 0.0 copy-start.4
  2.9 1.2 %fourier.1 = f32[32,4,128]{2,1,0:T(4,128)} custom-call(bf16[2048,128]{1,0:T(8,128)(2,1)S(1)} %bitcast.10, bf16[256,128]{1,0:T(8,128)(2,1)S(1)} %get-tuple-element.9.mask_ref, bf16[1,256,128]{2,1,0:T(8,128)(2,1)S(1)} %get-tuple-element.10.table_ref, f32[1,128,128]{2,1,0:T(8,128)S(1)} %get-tuple-element.11.turn_ref), custom_call_target="tpu_custom_call" | custom-call | tf_op jit(solution)/shard_map/fourier/pallas_call | solution.py:250
  4.2 7.3 %all-to-all-start = ((f32[32,4,128]{2,1,0:T(4,128)}), f32[32,4,128]{2,1,0:T(4,128)S(1)}, u32[]{:S(2)}, u32[]{:S(2)}) async-start(f32[32,4,128]{2,1,0:T(4,128)} %fourier.1), calls=%async_computation | async-start | bytes 131072 | tf_op jit(solution)/shard_map/all_to_all | solution.py:258
  11.5 0.0 copy-done.4
  11.5 0.1 reshape.17.legendre_ref
  11.6 7.3 %all-to-all-done.sums_ref = f32[32,4,128]{2,1,0:T(4,128)S(1)} async-done(((f32[32,4,128]{2,1,0:T(4,128)}), f32[32,4,128]{2,1,0:T(4,128)S(1)}, u32[]{:S(2)}, u32[]{:S(2)}) %all-to-all-start) | async-done | bytes 65568 | tf_op jit(solution)/shard_map/all_to_all | solution.py:258
  18.9 1.5 %legendre.1 = f32[512,128]{1,0:T(8,128)} custom-call(f32[32,4,128]{2,1,0:T(4,128)S(1)} %all-to-all-done.sums_ref, f32[4,8,128]{2,1,0:T(8,128)S(1)} %get-tuple-element.12.aux_ref, bf16[128,1024]{1,0:T(8,128)(2,1)S(1)} %reshape.17.legendre_ref), custom_call_target="tpu_custom_call" | custom-call | tf_op jit(solution)/shard_map/legendre/pallas_call | solution.py:260
Async XLA Ops:
  0.0 2.9 %copy-start = (bf16[8,2,4,4096]{3,2,1,0:T(4,128)(2,1)S(1)}, bf16[8,2,4,4096]{3,2,1,0:T(4,128)(2,1)}, u32[]{:S(2)}) copy-start(bf16[8,2,4,4096]{3,2,1,0:T(4,128)(2,1)} %param.5) | copy-start | bytes 1572868
  0.0 0.7 %copy-start.1 = (s32[2,4]{1,0:T(2,128)S(1)}, s32[2,4]{1,0:T(2,128)}, u32[]{:S(2)}) copy-start(s32[2,4]{1,0:T(2,128)} %start_ref.1) | copy-start | bytes 100
  0.7 0.7 %copy-start.2 = (s32[2,4]{1,0:T(2,128)S(1)}, s32[2,4]{1,0:T(2,128)}, u32[]{:S(2)}) copy-start(s32[2,4]{1,0:T(2,128)} %count_ref.1) | copy-start | bytes 100
  1.4 0.7 %copy-start.3 = (s32[32]{0:T(128)S(1)}, s32[32]{0:T(128)}, u32[]{:S(2)}) copy-start(s32[32]{0:T(128)} %modes_ref.1) | copy-start | bytes 388
  2.9 8.6 %copy-start.4 = (bf16[4,8,4,1024]{3,2,1,0:T(4,128)(2,1)S(1)}, bf16[4,8,4,1024]{3,2,1,0:T(4,128)(2,1)}, u32[]{:S(2)}) copy-start(bf16[4,8,4,1024]{3,2,1,0:T(4,128)(2,1)} %param.9) | copy-start | bytes 786436
  4.2 14.7 %all-to-all-start = ((f32[32,4,128]{2,1,0:T(4,128)}), f32[32,4,128]{2,1,0:T(4,128)S(1)}, u32[]{:S(2)}, u32[]{:S(2)}) async-start(f32[32,4,128]{2,1,0:T(4,128)} %fourier.1), calls=%async_computation | async-start | bytes 131072 | tf_op jit(solution)/shard_map/all_to_all | solution.py:258

commit v3 on v2

--- a/solution.py
+++ b/solution.py
@@ -10,7 +10,6 @@
 DIFFUSION = 0.2
 LANES = 128
 STEP = 4
-ROOM = pltpu.CompilerParams(vmem_limit_bytes=28 * 2**20)
 
 COS_TERMS = (1.0, -1.0 / 2, 1.0 / 24, -1.0 / 720, 1.0 / 40320, -1.0 / 3628800)
 SIN_TERMS = (1.0, -1.0 / 6, 1.0 / 120, -1.0 / 5040, 1.0 / 362880)
@@ -228,6 +227,7 @@
     ring = quarter * copies
     chunk = min(slots, LANES // 4)
     chunks = slots // chunk
+    room = pltpu.CompilerParams(vmem_limit_bytes=28 * 2**20 if chunks > 1 else None)
     pieces = quarter // LANES
     sky_rows = sky.reshape(maps, 2, band, pieces, LANES).transpose(0, 1, 3, 2, 4)
     sky_rows = sky_rows.reshape(maps * 2 * pieces * band, LANES)
@@ -244,7 +244,7 @@
         in_specs=[scalars] * 3,
         out_specs=(whole,) * 4,
         cost_estimate=pl.CostEstimate(flops=10**9, bytes_accessed=4 * 10**6, transcendentals=10**6),
-        compiler_params=ROOM,
+        compiler_params=room,
         name="tables",
     )(arc_start, arc_count, owner_modes)
     partial = pl.pallas_call(
@@ -252,19 +252,21 @@
         out_shape=pltpu.VMEM((blocks * copies, owned, LANES), jnp.float32),
         in_specs=[whole] * 4,
         out_specs=whole,
-        compiler_params=ROOM,
+        compiler_params=room,
         name="fourier",
     )(*(on_chip(v) for v in (sky_rows, mask, table, turn)))
     received = lax.all_to_all(partial, ("blk", "lblk"), split_axis=0, concat_axis=0, tiled=True)
+    legendre, received = lax.optimization_barrier((legendre, received))
+    legendre_rows = legendre.reshape(owned * groups * band, degrees)
     columns = degrees // LANES
     result = pl.pallas_call(
         legendre_kernel(maps, band, owned, blocks, copies, degrees, ring),
         out_shape=jax.ShapeDtypeStruct((maps * 2 * columns * owned, LANES), jnp.float32),
         in_specs=[whole] * 3,
         out_specs=whole,
-        compiler_params=ROOM,
+        compiler_params=room,
         name="legendre",
-    )(on_chip(received), on_chip(aux), on_chip(legendre.reshape(owned * groups * band, degrees)))
+    )(on_chip(received), on_chip(aux), on_chip(legendre_rows))
     result = result.reshape(maps, 2, columns, owned, LANES).transpose(0, 1, 3, 2, 4)
     return result.reshape(maps, 2, owned, degrees)
 

time: 20.6 us -> 18 us (0.87)
  blocking collectives: 0 us -> 14.5 us
  waiting for transfers between devices: 7.33 us -> 0 us
  starting transfers between devices: 7.32 us -> 0 us
  local copies, waits for them, and re-layouts: 2.14 us -> 0.07 us
  Pallas kernels: 3.53 us -> 3.15 us
    all_to_all x0 -> x1, blocking collectives: none -> 14.5 us  [local(): lax.all_to_all(partial, ('blk', 'lblk'), split_axis=0, concat_axis=0, til...]
    all_to_all x1 -> x0, waiting for transfers between devices: 7.33 us -> none  [local(): lax.all_to_all(partial, ('blk', 'lblk'), split_axis=0, concat_axis=0, til...]
    all_to_all x1 -> x0, starting transfers between devices: 7.32 us -> none  [local(): lax.all_to_all(partial, ('blk', 'lblk'), split_axis=0, concat_axis=0, til...]
    unnamed x10 -> x4, local copies, waits for them, and re-layouts: 2.08 us -> 0.01 us
    pallas_call x1, Pallas kernels: 1.24 us -> 0.59 us  [local(): pl.pallas_call(fourier_kernel(maps, band, pieces, owned, copies, chunk, c...]
    pallas_call x1, Pallas kernels: 0.84 us -> 1.11 us  [local(): pl.pallas_call(table_kernel(band, quarter, ring, owned, chunk), out_shape...]
  transfers between devices with their start and end apart: 1 -> 0, of which waited for: 1 -> 0; matrix products, arithmetic and copies ran while one was open for 0% -> 0% of each run, Pallas kernels for 0% -> 0%
where the time goes in v3:
time: 18 us; the launch traced here: 17.8 us
  blocking collectives  14.5 us (81%)
  Pallas kernels  3.15 us (18%)
    all_to_all x1, blocking collectives, local(): lax.all_to_all(partial, ('blk', 'lblk'), split_axis=0, concat_axis=0, til...  14.5 us
    pallas_call x1, Pallas kernels, local(): pl.pallas_call(legendre_kernel(maps, band, owned, blocks, copies, degrees...  1.45 us
    pallas_call x1, Pallas kernels, local(): pl.pallas_call(table_kernel(band, quarter, ring, owned, chunk), out_shape...  1.11 us
    pallas_call x1, Pallas kernels, local(): pl.pallas_call(fourier_kernel(maps, band, pieces, owned, copies, chunk, c...  0.59 us

profile of v3, /device:TPU:0, one launch (start us, length us, event | category | flops | bytes accessed | tf_op | source)
XLA Modules:
  0.0 17.8 jit_solution(6716467214996308154)
XLA Ops:
  0.0 0.0 copy-start
  0.0 1.1 %tables.1 = (bf16[256,128]{1,0:T(8,128)(2,1)S(1)}, bf16[1,256,128]{2,1,0:T(8,128)(2,1)S(1)}, f32[1,128,128]{2,1,0:T(8,128)S(1)}, f32[4,8,128]{2,1,0:T(8,128)S(1)}) custom-call(s32[2,4]{1,0:T(2,128)} %start_ref.1, s32[2,4]{1,0:T(2,128)} %count_ref.1, s32[32]{0:T(128)} %modes_ref.1), custom_call_target="tpu_custom_call" | custom-call | flops 1000000000 | bytes 4000000 | tf_op jit(solution)/shard_map/tables/pallas_call | solution.py:236
  1.1 0.0 copy-done
  1.1 0.0 copy-start.1
  1.1 0.6 %fourier.1 = f32[32,4,128]{2,1,0:T(4,128)S(1)} custom-call(bf16[2048,128]{1,0:T(8,128)(2,1)S(1)} %bitcast.10, bf16[256,128]{1,0:T(8,128)(2,1)S(1)} %get-tuple-element.11.mask_ref, bf16[1,256,128]{2,1,0:T(8,128)(2,1)S(1)} %get-tuple-element.12.table_ref, f32[1,128,128]{2,1,0:T(8,128)S(1)} %get-tuple-element.13.turn_ref), custom_call_target="tpu_custom_call" | custom-call | tf_op jit(solution)/shard_map/fourier/pallas_call | solution.py:250
  1.7 14.5 %all_to_all.5.sums_ref = f32[32,4,128]{2,1,0:T(4,128)S(1)} all-to-all(f32[32,4,128]{2,1,0:T(4,128)S(1)} %fourier.1), channel_id=1, replica_groups=mesh['blk'=8,'lblk'=4] {'blk','lblk'}, dimensions={0} | all-to-all | bytes 131072 | tf_op jit(solution)/shard_map/all_to_all | solution.py:258
  16.3 0.0 copy-done.1
  16.3 0.1 reshape.17.legendre_ref
  16.4 1.4 %legendre.1 = f32[512,128]{1,0:T(8,128)} custom-call(f32[32,4,128]{2,1,0:T(4,128)S(1)} %all_to_all.5.sums_ref, f32[4,8,128]{2,1,0:T(8,128)S(1)} %get-tuple-element.15.aux_ref, bf16[128,1024]{1,0:T(8,128)(2,1)S(1)} %reshape.17.legendre_ref), custom_call_target="tpu_custom_call" | custom-call | tf_op jit(solution)/shard_map/legendre/pallas_call | solution.py:262
Async XLA Ops:
  0.0 1.1 %copy-start = (bf16[8,2,4,4096]{3,2,1,0:T(4,128)(2,1)S(1)}, bf16[8,2,4,4096]{3,2,1,0:T(4,128)(2,1)}, u32[]{:S(2)}) copy-start(bf16[8,2,4,4096]{3,2,1,0:T(4,128)(2,1)} %param.5) | copy-start | bytes 1572868
  1.1 15.2 %copy-start.1 = (bf16[4,8,4,1024]{3,2,1,0:T(4,128)(2,1)S(1)}, bf16[4,8,4,1024]{3,2,1,0:T(4,128)(2,1)}, u32[]{:S(2)}) copy-start(bf16[4,8,4,1024]{3,2,1,0:T(4,128)(2,1)} %param.9) | copy-start | bytes 786436

commit v4 on v3

v4 whole, which is shorter than its diff:
```python
import math

import jax
import jax.numpy as jnp
from jax import lax
from jax.experimental import pallas as pl
from jax.experimental.pallas import tpu as pltpu
from jax.sharding import PartitionSpec as P

DIFFUSION = 0.2
LANES = 128
STEP = 4

COS_TERMS = (1.0, -1.0 / 2, 1.0 / 24, -1.0 / 720, 1.0 / 40320, -1.0 / 3628800)
SIN_TERMS = (1.0, -1.0 / 6, 1.0 / 120, -1.0 / 5040, 1.0 / 362880)


def horner(terms, square):
    total = jnp.full_like(square, terms[-1])
    for term in terms[-2::-1]:
        total = total * square + term
    return total


def circle(index, turn):
    index = index & (turn - 1)
    quadrant = (index * 4 + turn // 2) >> (turn.bit_length() - 1)
    rest = (index - quadrant * (turn // 4)).astype(jnp.float32) * (2.0 * math.pi / turn)
    square = rest * rest
    cosine = horner(COS_TERMS, square)
    sine = rest * horner(SIN_TERMS, square)
    odd = (quadrant & 1) == 1
    swapped_cos = jnp.where(odd, sine, cosine)
    swapped_sin = jnp.where(odd, cosine, sine)
    cos_sign = ((quadrant + 1) & 2) == 2
    sin_sign = (quadrant & 2) == 2
    return (
        jnp.where(cos_sign, -swapped_cos, swapped_cos),
        jnp.where(sin_sign, -swapped_sin, swapped_sin),
    )


def iota(shape, axis):
    return lax.broadcasted_iota(jnp.int32, shape, axis)


def powers(first, count):
    return [first << i for i in range(count.bit_length() - 1)]


def rotations(index, lane_modes, ring):
    amount = jnp.zeros((len(index), 1), jnp.int32)
    for i, value in enumerate(index):
        amount = jnp.where(iota(amount.shape, 0) == i, value, amount)
    return circle(amount * lane_modes, ring)


def unrolled(first, second, cosines, sines):
    blocks = [(first, second)]
    for i in range(cosines.shape[0]):
        cosine, sine = cosines[i : i + 1], sines[i : i + 1]
        blocks += [(f * cosine - s * sine, s * cosine + f * sine) for f, s in blocks]
    return [f for f, _ in blocks]


def table_kernel(band, quarter, ring, owned, chunk):
    pieces = quarter // LANES
    width = 4 * chunk

    def body(start_ref, count_ref, modes_ref, lane_modes_ref, mask_ref, table_ref, turn_ref, aux_ref):
        first_pixel = lax.axis_index("lblk") * quarter
        block = lax.axis_index("blk")
        row = iota((8, LANES), 0)
        lane = iota((8, LANES), 1)
        mine = jnp.zeros((8, LANES), jnp.int32)
        for s in range(owned):
            mine = jnp.where(row % owned == s, modes_ref[block * owned + s], mine)
        half = LANES // 2
        odd = (lane // (half // band)) % band % 2
        scale = DIFFUSION / math.sqrt(ring)
        step_cos, _ = circle(mine, ring)
        turn_cos, turn_sin = circle(mine * odd, 2 * ring)
        turn_sin = jnp.where(lane < half, turn_sin, -turn_sin)
        centre = scale * (1.0 + 2.0 * step_cos)
        aux_ref[0] = turn_cos * centre
        aux_ref[1] = turn_cos * scale
        aux_ref[2] = turn_sin * centre
        aux_ref[3] = turn_sin * scale
        aux_ref[4] = mine.astype(jnp.float32)

        masks = []
        for h in range(2):
            start = jnp.zeros((8, LANES), jnp.int32)
            count = jnp.zeros((8, LANES), jnp.int32)
            for k in range(band):
                start = jnp.where(row % band == k, start_ref[h, k], start)
                count = jnp.where(row % band == k, count_ref[h, k], count)
            shifted = first_pixel + (row // band) * LANES + lane - start
            for t in range(pieces * band // 8):
                offset = (shifted + t * (8 // band) * LANES) & (ring - 1)
                masks.append(jnp.where(offset < count, 1.0, 0.0))
        mask_ref[...] = jnp.concatenate(masks, axis=0).astype(jnp.bfloat16)

        kind = iota((1, width), 1) // chunk
        step = 8 // band * LANES
        in_table = powers(8, LANES // 8)
        in_turn = powers(step, quarter // step)
        for g in range(lane_modes_ref.shape[0]):
            modes = jnp.concatenate([lane_modes_ref[g]] * 4, axis=1)
            cosines, sines = rotations(in_table + in_turn, modes, ring)
            cosine, sine = circle(iota((8, width), 0) * modes, ring)
            is_cos = kind % 2 == 0
            blocks = unrolled(
                jnp.where(is_cos, cosine, sine),
                jnp.where(is_cos, sine, -cosine),
                cosines[: len(in_table)],
                sines[: len(in_table)],
            )
            table = jnp.concatenate(blocks, axis=0)
            high = table.astype(jnp.bfloat16)
            table_ref[g, :LANES] = high
            table_ref[g, LANES:] = (table - high.astype(jnp.float32)).astype(jnp.bfloat16)
            pixel = first_pixel + iota((8, width), 0) // band * LANES
            cosine, sine = circle(pixel * modes, ring)
            blocks = unrolled(
                jnp.where(kind == 0, cosine, jnp.where(kind == 3, -cosine, -sine)),
                jnp.where(kind == 0, sine, jnp.where(kind == 3, -sine, cosine)),
                cosines[len(in_table) :],
                sines[len(in_table) :],
            )
            turn_ref[g] = jnp.concatenate(blocks, axis=0)

    return body


def fourier_kernel(maps, band, pieces, owned, copies, chunk, chunks, step):
    rows = 2 * pieces * band
    tiles = pieces * band // 8
    lines = 2 * maps
    group = 8 // owned

    def body(sky_ref, mask_ref, table_ref, turn_ref, out_ref, line_ref):
        lower = iota((8, LANES), 0) < owned

        def run(g):
            for first in range(0, maps, step):
                values = [
                    sky_ref[x * rows : (x + 1) * rows] * mask_ref[...]
                    for x in range(first, first + step)
                ]
                values = jnp.concatenate(values, axis=0)
                wide = jnp.concatenate([values, values], axis=1)
                product = jnp.dot(wide, table_ref[g], preferred_element_type=jnp.float32)
                for x in range(step):
                    totals = []
                    for h in range(2):
                        total = None
                        for t in range(tiles):
                            at = ((x * 2 + h) * tiles + t) * 8
                            term = product[at : at + 8] * turn_ref[g, t * 8 : t * 8 + 8]
                            total = term if total is None else total + term
                        totals.append(total)
                    north, south = totals
                    line_ref[pl.ds(first + x, 8, stride=lines)] = north + south
                    line_ref[pl.ds(maps + first + x, 8, stride=lines)] = north - south
            gathered = line_ref[: band * lines]
            for piece in range(1, 8 // band):
                gathered = gathered + line_ref[piece * band * lines : (piece + 1) * band * lines]
            turned = gathered.T
            real = turned[:chunk] + turned[chunk : 2 * chunk]
            imag = turned[2 * chunk : 3 * chunk] + turned[3 * chunk :]
            both = jnp.concatenate([real, imag], axis=1)
            tile = copies // group
            for i in range(chunk // 8):
                value = both[i * 8 : i * 8 + 8]
                other = pltpu.roll(value, owned, 0)
                ready = (jnp.where(lower, value, other), jnp.where(lower, other, value))
                for o in range(group):
                    for c in range(tile):
                        at = ((g * (chunk // 8) + i) * group + o) * tile + c
                        out_ref[pl.ds(at * 8, 8)] = ready[o]

        if chunks == 1:
            run(0)
        else:
            lax.fori_loop(0, chunks, lambda g, _: run(g), None)

    return body


def legendre_kernel(maps, band, owned, blocks, copies, degrees, ring):
    cycles = blocks * band
    depth = owned * cycles
    lines = 2 * maps
    half = LANES // 2
    tile = copies * owned // 8
    columns = degrees // LANES

    def body(sums_ref, aux_ref, legendre_ref, out_ref):
        lane = iota((8, LANES), 1)
        lower = iota((8, LANES), 0) < owned
        cycle = lane // lines % band
        is_first = cycle == 0
        is_last = cycle == band - 1
        mirror = jnp.where(lane // maps % 2 == 0, 1.0, -1.0)

        single = []
        for b in range(blocks):
            total = sums_ref[b * tile * 8 : b * tile * 8 + 8]
            for i in range(1, tile):
                total = total + sums_ref[(b * tile + i) * 8 : (b * tile + i) * 8 + 8]
            single.append(total + pltpu.roll(total, owned, 0))
        none = jnp.zeros((8, LANES), jnp.float32)

        def pair(b):
            at = lambda i: single[i] if 0 <= i < blocks else none
            return jnp.where(lower, at(b), at(b + 1))

        def moved(value, shift):
            return pltpu.roll(value, shift % LANES, 1)

        folded = []
        for b in range(0, blocks, 2):
            here = pair(b)
            prior = jnp.where(is_last, pair(b - 1), here)
            later = jnp.where(is_first, pair(b + 1), here)
            swapped = moved(here, half)
            up, up_swapped = moved(prior, lines), moved(prior, lines + half)
            down, down_swapped = moved(later, -lines), moved(later, half - lines)
            above = jnp.where(is_first, up_swapped, up)
            above_swapped = jnp.where(is_first, up, up_swapped)
            below = jnp.where(is_last, down_swapped, down)
            below_swapped = jnp.where(is_last, down, down_swapped)
            if b + 2 == blocks:
                equator = is_last & ~lower
                below = jnp.where(equator, mirror * here, below)
                below_swapped = jnp.where(equator, mirror * swapped, below_swapped)
            folded.append(
                aux_ref[0] * here
                + aux_ref[1] * (above + below)
                + aux_ref[2] * swapped
                + aux_ref[3] * (above_swapped + below_swapped)
            )
        folded = jnp.concatenate(folded, axis=0).astype(jnp.bfloat16)

        row = iota((blocks * owned, depth), 0)
        column = iota((blocks * owned, depth), 1)
        spread = (row // owned == (column // band) % blocks) & (row % owned == column // cycles)
        spread = jnp.where(spread, 1.0, 0.0).astype(jnp.bfloat16)
        across = lax.dot_general(
            folded, spread, (((0,), (0,)), ((), ())), preferred_element_type=jnp.float32
        )
        column = iota((lines, depth), 1)
        parts = []
        for part in range(2):
            chosen = across[part * half : part * half + lines]
            for k in range(1, band):
                at = part * half + k * lines
                chosen = jnp.where(column % band == k, across[at : at + lines], chosen)
            parts.append(chosen)
        weights = []
        for s in range(owned):
            for part in range(2):
                weights.append(jnp.where(column // cycles == s, parts[part], 0.0))
        weights = jnp.concatenate(weights, axis=0).astype(jnp.bfloat16)
        sums = jnp.dot(weights, legendre_ref[...], preferred_element_type=jnp.float32)

        first = lax.axis_index("lblk") * degrees
        for s in range(owned):
            mode = jnp.broadcast_to(aux_ref[4, s : s + 1], (maps, LANES)).astype(jnp.int32)
            degree = first + iota((maps, LANES), 1)
            even = ((degree + mode) & 1) == 0
            beyond = degree - mode
            for j in range(columns):
                inside = beyond >= -j * LANES
                for part in range(2):
                    at = (s * 2 + part) * lines
                    plus = sums[at : at + maps, j * LANES : (j + 1) * LANES]
                    minus = sums[at + maps : at + lines, j * LANES : (j + 1) * LANES]
                    value = jnp.where(inside, jnp.where(even, plus, minus), 0.0)
                    at = (part * columns + j) * owned + s
                    out_ref[pl.ds(at, maps, stride=2 * columns * owned)] = value

    return body


def on_chip(value):
    return pltpu.with_memory_space_constraint(value, pltpu.VMEM)


def local(sky, arc_start, arc_count, owner_modes, legendre):
    maps, _, band, quarter = sky.shape
    slots = owner_modes.shape[0]
    owned, groups, _, degrees = legendre.shape
    blocks, copies = lax.axis_size("blk"), lax.axis_size("lblk")
    ring = quarter * copies
    chunk = min(slots, LANES // 4)
    chunks = slots // chunk
    room = pltpu.CompilerParams(vmem_limit_bytes=28 * 2**20 if chunks > 1 else None)
    pieces = quarter // LANES
    sky_rows = sky.reshape(maps, 2, band, pieces, LANES).transpose(0, 1, 3, 2, 4)
    sky_rows = sky_rows.reshape(maps * 2 * pieces * band, LANES)
    scalars = pl.BlockSpec(memory_space=pltpu.SMEM)
    whole = pl.BlockSpec(memory_space=pltpu.VMEM)
    mask, table, turn, aux = pl.pallas_call(
        table_kernel(band, quarter, ring, owned, chunk),
        out_shape=(
            pltpu.VMEM((2 * pieces * band, LANES), jnp.bfloat16),
            pltpu.VMEM((chunks, 2 * LANES, 4 * chunk), jnp.bfloat16),
            pltpu.VMEM((chunks, pieces * band, 4 * chunk), jnp.float32),
            pltpu.VMEM((5, 8, LANES), jnp.float32),
        ),
        in_specs=[scalars] * 3 + [whole],
        out_specs=(whole,) * 4,
        cost_estimate=pl.CostEstimate(flops=10**9, bytes_accessed=4 * 10**6, transcendentals=10**6),
        compiler_params=room,
        name="tables",
    )(arc_start, arc_count, owner_modes, owner_modes.reshape(chunks, 1, chunk))
    partial = pl.pallas_call(
        fourier_kernel(maps, band, pieces, owned, copies, chunk, chunks, STEP),
        out_shape=pltpu.VMEM((blocks * copies * owned, LANES), jnp.float32),
        in_specs=[whole] * 4,
        out_specs=whole,
        scratch_shapes=[pltpu.VMEM((8 * 2 * maps, LANES), jnp.float32)],
        compiler_params=room,
        name="fourier",
    )(*(on_chip(v) for v in (sky_rows, mask, table, turn)))
    partial = partial.reshape(blocks * copies, owned, LANES)
    received = lax.all_to_all(partial, ("blk", "lblk"), split_axis=0, concat_axis=0, tiled=True)
    legendre, received = lax.optimization_barrier((legendre, received))
    legendre_rows = legendre.reshape(owned * groups * band, degrees)
    received = received.reshape(blocks * copies * owned, LANES)
    columns = degrees // LANES
    result = pl.pallas_call(
        legendre_kernel(maps, band, owned, blocks, copies, degrees, ring),
        out_shape=jax.ShapeDtypeStruct((maps * 2 * columns * owned, LANES), jnp.float32),
        in_specs=[whole] * 3,
        out_specs=whole,
        compiler_params=room,
        name="legendre",
    )(on_chip(received), on_chip(aux), on_chip(legendre_rows))
    result = result.reshape(maps, 2, columns, owned, LANES).transpose(0, 1, 3, 2, 4)
    return result.reshape(maps, 2, owned, degrees)


def solution(mesh):
    return jax.shard_map(
        local,
        mesh=mesh,
        in_specs=(
            P(None, None, "blk", "lblk"),
            P(None, "blk"),
            P(None, "blk"),
            P(),
            P("blk", None, None, "lblk"),
        ),
        out_specs=P(None, None, "blk", "lblk"),
        check_vma=False,
    )
```

time: 18 us -> 17.7 us (0.983)
  Pallas kernels: 3.15 us -> 2.84 us
    pallas_call x1, Pallas kernels: 1.45 us -> 1.27 us  [local(): pl.pallas_call(legendre_kernel(maps, band, owned, blocks, copies, degrees...]
where the time goes in v4:
time: 17.7 us; the launch traced here: 17.6 us
  blocking collectives  14.5 us (82%)
  Pallas kernels  2.84 us (16%)
    all_to_all x1, blocking collectives, local(): lax.all_to_all(partial, ('blk', 'lblk'), split_axis=0, concat_axis=0, til...  14.5 us
    pallas_call x1, Pallas kernels, local(): pl.pallas_call(legendre_kernel(maps, band, owned, blocks, copies, degrees...  1.27 us
    pallas_call x1, Pallas kernels, local(): pl.pallas_call(table_kernel(band, quarter, ring, owned, chunk), out_shape...  0.97 us
    pallas_call x1, Pallas kernels, local(): pl.pallas_call(fourier_kernel(maps, band, pieces, owned, copies, chunk, c...  0.61 us

profile of v4, /device:TPU:0, one launch (start us, length us, event | category | flops | bytes accessed | tf_op | source)
XLA Modules:
  0.0 17.6 jit_solution(14558125425498368127)
XLA Ops:
  0.0 0.0 copy-start
  0.0 1.0 %tables.1 = (bf16[256,128]{1,0:T(8,128)(2,1)S(1)}, bf16[1,256,128]{2,1,0:T(8,128)(2,1)S(1)}, f32[1,128,128]{2,1,0:T(8,128)S(1)}, f32[5,8,128]{2,1,0:T(8,128)S(1)}) custom-call(s32[2,4]{1,0:T(2,128)} %start_ref.1, s32[2,4]{1,0:T(2,128)} %count_ref.1, s32[32]{0:T(128)} %modes_ref.1, s32[1,1,32]{2,1,0:T(1,128)} %bitcast.16), custom_call_target="tpu_custom_call" | custom-call | flops 1000000000 | bytes 4000000 | tf_op jit(solution)/shard_map/tables/pallas_call | solution.py:305
  1.0 0.1 copy-done
  1.1 0.0 copy-start.1
  1.1 0.6 %fourier.1 = f32[128,128]{1,0:T(8,128)S(1)} custom-call(bf16[2048,128]{1,0:T(8,128)(2,1)S(1)} %bitcast.13, bf16[256,128]{1,0:T(8,128)(2,1)S(1)} %get-tuple-element.11.mask_ref, bf16[1,256,128]{2,1,0:T(8,128)(2,1)S(1)} %get-tuple-element.12.table_ref, f32[1,128,128]{2,1,0:T(8,128)S(1)} %get-tuple-element.13.turn_ref), custom_call_target="tpu_custom_call" | custom-call | tf_op jit(solution)/shard_map/fourier/pallas_call | solution.py:319
  1.7 14.5 %all_to_all.5 = f32[32,4,128]{2,1,0:T(4,128)S(1)} all-to-all(f32[32,4,128]{2,1,0:T(4,128)S(1)} %bitcast.15), channel_id=1, replica_groups=mesh['blk'=8,'lblk'=4] {'blk','lblk'}, dimensions={0} | all-to-all | bytes 131072 | tf_op jit(solution)/shard_map/all_to_all | solution.py:329
  16.2 0.0 copy-done.1
  16.2 0.1 reshape.29.legendre_ref
  16.3 1.3 %legendre.1 = f32[512,128]{1,0:T(8,128)} custom-call(f32[128,128]{1,0:T(8,128)S(1)} %bitcast.14, f32[5,8,128]{2,1,0:T(8,128)S(1)} %get-tuple-element.15.aux_ref, bf16[128,1024]{1,0:T(8,128)(2,1)S(1)} %reshape.29.legendre_ref), custom_call_target="tpu_custom_call" | custom-call | tf_op jit(solution)/shard_map/legendre/pallas_call | solution.py:334
Async XLA Ops:
  0.0 1.1 %copy-start = (bf16[8,2,4,4096]{3,2,1,0:T(4,128)(2,1)S(1)}, bf16[8,2,4,4096]{3,2,1,0:T(4,128)(2,1)}, u32[]{:S(2)}) copy-start(bf16[8,2,4,4096]{3,2,1,0:T(4,128)(2,1)} %param.5) | copy-start | bytes 1572868
  1.1 15.2 %copy-start.1 = (bf16[4,8,4,1024]{3,2,1,0:T(4,128)(2,1)S(1)}, bf16[4,8,4,1024]{3,2,1,0:T(4,128)(2,1)}, u32[]{:S(2)}) copy-start(bf16[4,8,4,1024]{3,2,1,0:T(4,128)(2,1)} %param.9) | copy-start | bytes 786436

commit v5 on v4

--- a/solution.py
+++ b/solution.py
@@ -116,10 +116,7 @@
                 cosines[: len(in_table)],
                 sines[: len(in_table)],
             )
-            table = jnp.concatenate(blocks, axis=0)
-            high = table.astype(jnp.bfloat16)
-            table_ref[g, :LANES] = high
-            table_ref[g, LANES:] = (table - high.astype(jnp.float32)).astype(jnp.bfloat16)
+            table_ref[g] = jnp.concatenate(blocks, axis=0).astype(jnp.bfloat16)
             pixel = first_pixel + iota((8, width), 0) // band * LANES
             cosine, sine = circle(pixel * modes, ring)
             blocks = unrolled(
@@ -144,22 +141,23 @@
 
         def run(g):
             for first in range(0, maps, step):
-                values = [
+                masked = [
                     sky_ref[x * rows : (x + 1) * rows] * mask_ref[...]
                     for x in range(first, first + step)
                 ]
-                values = jnp.concatenate(values, axis=0)
-                wide = jnp.concatenate([values, values], axis=1)
-                product = jnp.dot(wide, table_ref[g], preferred_element_type=jnp.float32)
+                product = jnp.dot(
+                    jnp.concatenate(masked, axis=0), table_ref[g], preferred_element_type=jnp.float32
+                )
                 for x in range(step):
                     totals = []
                     for h in range(2):
-                        total = None
+                        terms = []
                         for t in range(tiles):
                             at = ((x * 2 + h) * tiles + t) * 8
-                            term = product[at : at + 8] * turn_ref[g, t * 8 : t * 8 + 8]
-                            total = term if total is None else total + term
-                        totals.append(total)
+                            terms.append(product[at : at + 8] * turn_ref[g, t * 8 : t * 8 + 8])
+                        while len(terms) > 1:
+                            terms = [a + b for a, b in zip(terms[::2], terms[1::2], strict=True)]
+                        totals += terms
                     north, south = totals
                     line_ref[pl.ds(first + x, 8, stride=lines)] = north + south
                     line_ref[pl.ds(maps + first + x, 8, stride=lines)] = north - south
@@ -196,7 +194,7 @@
     tile = copies * owned // 8
     columns = degrees // LANES
 
-    def body(sums_ref, aux_ref, legendre_ref, out_ref):
+    def body(sums_ref, aux_ref, legendre_ref, out_ref, line_ref):
         lane = iota((8, LANES), 1)
         lower = iota((8, LANES), 0) < owned
         cycle = lane // lines % band
@@ -258,28 +256,43 @@
                 at = part * half + k * lines
                 chosen = jnp.where(column % band == k, across[at : at + lines], chosen)
             parts.append(chosen)
+        for part in range(2):
+            line_ref[part * lines : (part + 1) * lines] = parts[part]
+        mine = iota((8, depth), 1) // cycles == iota((8, depth), 0) % owned
         weights = []
-        for s in range(owned):
-            for part in range(2):
-                weights.append(jnp.where(column // cycles == s, parts[part], 0.0))
+        for i in range(lines):
+            value = jnp.where(
+                iota((8, depth), 0) < owned,
+                line_ref[pl.ds(i, 8, stride=0)],
+                line_ref[pl.ds(lines + i, 8, stride=0)],
+            )
+            weights.append(jnp.where(mine, value, 0.0))
         weights = jnp.concatenate(weights, axis=0).astype(jnp.bfloat16)
         sums = jnp.dot(weights, legendre_ref[...], preferred_element_type=jnp.float32)
 
-        first = lax.axis_index("lblk") * degrees
-        for s in range(owned):
-            mode = jnp.broadcast_to(aux_ref[4, s : s + 1], (maps, LANES)).astype(jnp.int32)
-            degree = first + iota((maps, LANES), 1)
-            even = ((degree + mode) & 1) == 0
-            beyond = degree - mode
-            for j in range(columns):
-                inside = beyond >= -j * LANES
-                for part in range(2):
-                    at = (s * 2 + part) * lines
-                    plus = sums[at : at + maps, j * LANES : (j + 1) * LANES]
-                    minus = sums[at + maps : at + lines, j * LANES : (j + 1) * LANES]
-                    value = jnp.where(inside, jnp.where(even, plus, minus), 0.0)
-                    at = (part * columns + j) * owned + s
-                    out_ref[pl.ds(at, maps, stride=2 * columns * owned)] = value
+        mode = aux_ref[4].astype(jnp.int32)
+        degree = lax.axis_index("lblk") * degrees + lane
+        even = ((degree + mode) & 1) == 0
+        beyond = degree - mode
+        for j in range(0, columns, 2):
+            inside = [beyond >= -(j + i) * LANES for i in range(2)]
+            for x in range(maps):
+                near, far = (
+                    jnp.where(
+                        inside[i],
+                        jnp.where(
+                            even,
+                            sums[x * 8 : x * 8 + 8, (j + i) * LANES : (j + i + 1) * LANES],
+                            sums[(maps + x) * 8 : (maps + x) * 8 + 8, (j + i) * LANES : (j + i + 1) * LANES],
+                        ),
+                        0.0,
+                    )
+                    for i in range(2)
+                )
+                at = (x * 2 * columns + j) * owned
+                out_ref[pl.ds(at, 8)] = jnp.where(lower, near, pltpu.roll(far, owned, 0))
+                at += columns * owned
+                out_ref[pl.ds(at, 8)] = jnp.where(lower, pltpu.roll(near, owned, 0), far)
 
     return body
 
@@ -306,7 +319,7 @@
         table_kernel(band, quarter, ring, owned, chunk),
         out_shape=(
             pltpu.VMEM((2 * pieces * band, LANES), jnp.bfloat16),
-            pltpu.VMEM((chunks, 2 * LANES, 4 * chunk), jnp.bfloat16),
+            pltpu.VMEM((chunks, LANES, 4 * chunk), jnp.bfloat16),
             pltpu.VMEM((chunks, pieces * band, 4 * chunk), jnp.float32),
             pltpu.VMEM((5, 8, LANES), jnp.float32),
         ),
@@ -336,6 +349,7 @@
         out_shape=jax.ShapeDtypeStruct((maps * 2 * columns * owned, LANES), jnp.float32),
         in_specs=[whole] * 3,
         out_specs=whole,
+        scratch_shapes=[pltpu.VMEM((4 * maps, owned * groups * band), jnp.float32)],
         compiler_params=room,
         name="legendre",
     )(on_chip(received), on_chip(aux), on_chip(legendre_rows))

time: 17.7 us -> 17.5 us (0.989)
  Pallas kernels: 2.84 us -> 2.62 us
where the time goes in v5:
time: 17.5 us; the launch traced here: 17.3 us
  blocking collectives  14.5 us (83%)
  Pallas kernels  2.62 us (15%)
    all_to_all x1, blocking collectives, local(): lax.all_to_all(partial, ('blk', 'lblk'), split_axis=0, concat_axis=0, til...  14.5 us
    pallas_call x1, Pallas kernels, local(): pl.pallas_call(legendre_kernel(maps, band, owned, blocks, copies, degrees...  1.2 us
    pallas_call x1, Pallas kernels, local(): pl.pallas_call(table_kernel(band, quarter, ring, owned, chunk), out_shape...  0.96 us
    pallas_call x1, Pallas kernels, local(): pl.pallas_call(fourier_kernel(maps, band, pieces, owned, copies, chunk, c...  0.46 us

profile of v5, /device:TPU:0, one launch (start us, length us, event | category | flops | bytes accessed | tf_op | source)
XLA Modules:
  0.0 17.3 jit_solution(471408248042799666)
XLA Ops:
  0.0 0.0 copy-start
  0.0 1.0 %tables.1 = (bf16[256,128]{1,0:T(8,128)(2,1)S(1)}, bf16[1,128,128]{2,1,0:T(8,128)(2,1)S(1)}, f32[1,128,128]{2,1,0:T(8,128)S(1)}, f32[5,8,128]{2,1,0:T(8,128)S(1)}) custom-call(s32[2,4]{1,0:T(2,128)} %start_ref.1, s32[2,4]{1,0:T(2,128)} %count_ref.1, s32[32]{0:T(128)} %modes_ref.1, s32[1,1,32]{2,1,0:T(1,128)} %bitcast.16), custom_call_target="tpu_custom_call" | custom-call | flops 1000000000 | bytes 4000000 | tf_op jit(solution)/shard_map/tables/pallas_call | solution.py:318
  1.0 0.1 copy-done
  1.1 0.0 copy-start.1
  1.1 0.5 %fourier.1 = f32[128,128]{1,0:T(8,128)S(1)} custom-call(bf16[2048,128]{1,0:T(8,128)(2,1)S(1)} %bitcast.13, bf16[256,128]{1,0:T(8,128)(2,1)S(1)} %get-tuple-element.11.mask_ref, bf16[1,128,128]{2,1,0:T(8,128)(2,1)S(1)} %get-tuple-element.12.table_ref, f32[1,128,128]{2,1,0:T(8,128)S(1)} %get-tuple-element.13.turn_ref), custom_call_target="tpu_custom_call" | custom-call | tf_op jit(solution)/shard_map/fourier/pallas_call | solution.py:332
  1.5 14.5 %all_to_all.5 = f32[32,4,128]{2,1,0:T(4,128)S(1)} all-to-all(f32[32,4,128]{2,1,0:T(4,128)S(1)} %bitcast.15), channel_id=1, replica_groups=mesh['blk'=8,'lblk'=4] {'blk','lblk'}, dimensions={0} | all-to-all | bytes 131072 | tf_op jit(solution)/shard_map/all_to_all | solution.py:342
  16.1 0.0 copy-done.1
  16.1 0.1 reshape.29.legendre_ref
  16.1 1.2 %legendre.1 = f32[512,128]{1,0:T(8,128)} custom-call(f32[128,128]{1,0:T(8,128)S(1)} %bitcast.14, f32[5,8,128]{2,1,0:T(8,128)S(1)} %get-tuple-element.15.aux_ref, bf16[128,1024]{1,0:T(8,128)(2,1)S(1)} %reshape.29.legendre_ref), custom_call_target="tpu_custom_call" | custom-call | tf_op jit(solution)/shard_map/legendre/pallas_call | solution.py:347
Async XLA Ops:
  0.0 1.1 %copy-start = (bf16[8,2,4,4096]{3,2,1,0:T(4,128)(2,1)S(1)}, bf16[8,2,4,4096]{3,2,1,0:T(4,128)(2,1)}, u32[]{:S(2)}) copy-start(bf16[8,2,4,4096]{3,2,1,0:T(4,128)(2,1)} %param.5) | copy-start | bytes 1572868
  1.1 15.0 %copy-start.1 = (bf16[4,8,4,1024]{3,2,1,0:T(4,128)(2,1)S(1)}, bf16[4,8,4,1024]{3,2,1,0:T(4,128)(2,1)}, u32[]{:S(2)}) copy-start(bf16[4,8,4,1024]{3,2,1,0:T(4,128)(2,1)} %param.9) | copy-start | bytes 786436

commit v6 on v5

--- a/solution.py
+++ b/solution.py
@@ -263,8 +263,8 @@
         for i in range(lines):
             value = jnp.where(
                 iota((8, depth), 0) < owned,
-                line_ref[pl.ds(i, 8, stride=0)],
-                line_ref[pl.ds(lines + i, 8, stride=0)],
+                jnp.broadcast_to(line_ref[i : i + 1], (8, depth)),
+                jnp.broadcast_to(line_ref[lines + i : lines + i + 1], (8, depth)),
             )
             weights.append(jnp.where(mine, value, 0.0))
         weights = jnp.concatenate(weights, axis=0).astype(jnp.bfloat16)

time: 17.5 us -> 17.5 us (level)
  no operation moved by 1% of the time
where the time goes in v6:
time: 17.5 us; the launch traced here: 17.3 us
  blocking collectives  14.5 us (83%)
  Pallas kernels  2.62 us (15%)
    all_to_all x1, blocking collectives, local(): lax.all_to_all(partial, ('blk', 'lblk'), split_axis=0, concat_axis=0, til...  14.5 us
    pallas_call x1, Pallas kernels, local(): pl.pallas_call(legendre_kernel(maps, band, owned, blocks, copies, degrees...  1.2 us
    pallas_call x1, Pallas kernels, local(): pl.pallas_call(table_kernel(band, quarter, ring, owned, chunk), out_shape...  0.96 us
    pallas_call x1, Pallas kernels, local(): pl.pallas_call(fourier_kernel(maps, band, pieces, owned, copies, chunk, c...  0.46 us

profile of v6, /device:TPU:0, one launch (start us, length us, event | category | flops | bytes accessed | tf_op | source)
XLA Modules:
  0.0 17.3 jit_solution(1458315451976427768)
XLA Ops:
  0.0 0.0 copy-start
  0.0 1.0 %tables.1 = (bf16[256,128]{1,0:T(8,128)(2,1)S(1)}, bf16[1,128,128]{2,1,0:T(8,128)(2,1)S(1)}, f32[1,128,128]{2,1,0:T(8,128)S(1)}, f32[5,8,128]{2,1,0:T(8,128)S(1)}) custom-call(s32[2,4]{1,0:T(2,128)} %start_ref.1, s32[2,4]{1,0:T(2,128)} %count_ref.1, s32[32]{0:T(128)} %modes_ref.1, s32[1,1,32]{2,1,0:T(1,128)} %bitcast.16), custom_call_target="tpu_custom_call" | custom-call | flops 1000000000 | bytes 4000000 | tf_op jit(solution)/shard_map/tables/pallas_call | solution.py:318
  1.0 0.1 copy-done
  1.1 0.0 copy-start.1
  1.1 0.5 %fourier.1 = f32[128,128]{1,0:T(8,128)S(1)} custom-call(bf16[2048,128]{1,0:T(8,128)(2,1)S(1)} %bitcast.13, bf16[256,128]{1,0:T(8,128)(2,1)S(1)} %get-tuple-element.11.mask_ref, bf16[1,128,128]{2,1,0:T(8,128)(2,1)S(1)} %get-tuple-element.12.table_ref, f32[1,128,128]{2,1,0:T(8,128)S(1)} %get-tuple-element.13.turn_ref), custom_call_target="tpu_custom_call" | custom-call | tf_op jit(solution)/shard_map/fourier/pallas_call | solution.py:332
  1.5 14.5 %all_to_all.5 = f32[32,4,128]{2,1,0:T(4,128)S(1)} all-to-all(f32[32,4,128]{2,1,0:T(4,128)S(1)} %bitcast.15), channel_id=1, replica_groups=mesh['blk'=8,'lblk'=4] {'blk','lblk'}, dimensions={0} | all-to-all | bytes 131072 | tf_op jit(solution)/shard_map/all_to_all | solution.py:342
  16.1 0.0 copy-done.1
  16.1 0.1 reshape.29.legendre_ref
  16.1 1.2 %legendre.1 = f32[512,128]{1,0:T(8,128)} custom-call(f32[128,128]{1,0:T(8,128)S(1)} %bitcast.14, f32[5,8,128]{2,1,0:T(8,128)S(1)} %get-tuple-element.15.aux_ref, bf16[128,1024]{1,0:T(8,128)(2,1)S(1)} %reshape.29.legendre_ref), custom_call_target="tpu_custom_call" | custom-call | tf_op jit(solution)/shard_map/legendre/pallas_call | solution.py:347
Async XLA Ops:
  0.0 1.1 %copy-start = (bf16[8,2,4,4096]{3,2,1,0:T(4,128)(2,1)S(1)}, bf16[8,2,4,4096]{3,2,1,0:T(4,128)(2,1)}, u32[]{:S(2)}) copy-start(bf16[8,2,4,4096]{3,2,1,0:T(4,128)(2,1)} %param.5) | copy-start | bytes 1572868
  1.1 15.0 %copy-start.1 = (bf16[4,8,4,1024]{3,2,1,0:T(4,128)(2,1)S(1)}, bf16[4,8,4,1024]{3,2,1,0:T(4,128)(2,1)}, u32[]{:S(2)}) copy-start(bf16[4,8,4,1024]{3,2,1,0:T(4,128)(2,1)} %param.9) | copy-start | bytes 786436

commit v7 on v6

--- a/solution.py
+++ b/solution.py
@@ -268,7 +268,7 @@
             )
             weights.append(jnp.where(mine, value, 0.0))
         weights = jnp.concatenate(weights, axis=0).astype(jnp.bfloat16)
-        sums = jnp.dot(weights, legendre_ref[...], preferred_element_type=jnp.float32)
+        sums = jnp.dot(weights, legendre_ref[...].reshape(depth, degrees), preferred_element_type=jnp.float32)
 
         mode = aux_ref[4].astype(jnp.int32)
         degree = lax.axis_index("lblk") * degrees + lane
@@ -340,8 +340,7 @@
     )(*(on_chip(v) for v in (sky_rows, mask, table, turn)))
     partial = partial.reshape(blocks * copies, owned, LANES)
     received = lax.all_to_all(partial, ("blk", "lblk"), split_axis=0, concat_axis=0, tiled=True)
-    legendre, received = lax.optimization_barrier((legendre, received))
-    legendre_rows = legendre.reshape(owned * groups * band, degrees)
+    legendre_rows = legendre.reshape(owned * groups, band, degrees)
     received = received.reshape(blocks * copies * owned, LANES)
     columns = degrees // LANES
     result = pl.pallas_call(

time: 17.5 us -> 17.4 us (level)
  no operation moved by 1% of the time
where the time goes in v7:
time: 17.4 us; the launch traced here: 17.3 us
  blocking collectives  14.5 us (83%)
  Pallas kernels  2.62 us (15%)
    all_to_all x1, blocking collectives, local(): lax.all_to_all(partial, ('blk', 'lblk'), split_axis=0, concat_axis=0, til...  14.5 us
    pallas_call x1, Pallas kernels, local(): pl.pallas_call(legendre_kernel(maps, band, owned, blocks, copies, degrees...  1.2 us
    pallas_call x1, Pallas kernels, local(): pl.pallas_call(table_kernel(band, quarter, ring, owned, chunk), out_shape...  0.96 us
    pallas_call x1, Pallas kernels, local(): pl.pallas_call(fourier_kernel(maps, band, pieces, owned, copies, chunk, c...  0.46 us

profile of v7, /device:TPU:0, one launch (start us, length us, event | category | flops | bytes accessed | tf_op | source)
XLA Modules:
  0.0 17.3 jit_solution(7954586374607607243)
XLA Ops:
  0.0 0.0 copy-start
  0.0 1.0 %tables.1 = (bf16[256,128]{1,0:T(8,128)(2,1)S(1)}, bf16[1,128,128]{2,1,0:T(8,128)(2,1)S(1)}, f32[1,128,128]{2,1,0:T(8,128)S(1)}, f32[5,8,128]{2,1,0:T(8,128)S(1)}) custom-call(s32[2,4]{1,0:T(2,128)} %start_ref.1, s32[2,4]{1,0:T(2,128)} %count_ref.1, s32[32]{0:T(128)} %modes_ref.1, s32[1,1,32]{2,1,0:T(1,128)} %bitcast.18), custom_call_target="tpu_custom_call" | custom-call | flops 1000000000 | bytes 4000000 | tf_op jit(solution)/shard_map/tables/pallas_call | solution.py:318
  1.0 0.1 copy-done
  1.1 0.0 copy-start.1
  1.1 0.5 %fourier.1 = f32[128,128]{1,0:T(8,128)S(1)} custom-call(bf16[2048,128]{1,0:T(8,128)(2,1)S(1)} %bitcast.14, bf16[256,128]{1,0:T(8,128)(2,1)S(1)} %get-tuple-element.9.mask_ref, bf16[1,128,128]{2,1,0:T(8,128)(2,1)S(1)} %get-tuple-element.10.table_ref, f32[1,128,128]{2,1,0:T(8,128)S(1)} %get-tuple-element.11.turn_ref), custom_call_target="tpu_custom_call" | custom-call | tf_op jit(solution)/shard_map/fourier/pallas_call | solution.py:332
  1.5 14.5 %all_to_all.5 = f32[32,4,128]{2,1,0:T(4,128)S(1)} all-to-all(f32[32,4,128]{2,1,0:T(4,128)S(1)} %bitcast.16), channel_id=1, replica_groups=mesh['blk'=8,'lblk'=4] {'blk','lblk'}, dimensions={0} | all-to-all | bytes 131072 | tf_op jit(solution)/shard_map/all_to_all | solution.py:342
  16.1 0.0 copy-done.1
  16.1 1.2 %legendre.1 = f32[512,128]{1,0:T(8,128)} custom-call(f32[128,128]{1,0:T(8,128)S(1)} %bitcast.17, f32[5,8,128]{2,1,0:T(8,128)S(1)} %get-tuple-element.12.aux_ref, bf16[32,4,1024]{2,1,0:T(4,128)(2,1)S(1)} %bitcast.15), custom_call_target="tpu_custom_call" | custom-call | tf_op jit(solution)/shard_map/legendre/pallas_call | solution.py:346
Async XLA Ops:
  0.0 1.1 %copy-start = (bf16[8,2,4,4096]{3,2,1,0:T(4,128)(2,1)S(1)}, bf16[8,2,4,4096]{3,2,1,0:T(4,128)(2,1)}, u32[]{:S(2)}) copy-start(bf16[8,2,4,4096]{3,2,1,0:T(4,128)(2,1)} %param.5) | copy-start | bytes 1572868
  1.1 15.0 %copy-start.1 = (bf16[4,8,4,1024]{3,2,1,0:T(4,128)(2,1)S(1)}, bf16[4,8,4,1024]{3,2,1,0:T(4,128)(2,1)}, u32[]{:S(2)}) copy-start(bf16[4,8,4,1024]{3,2,1,0:T(4,128)(2,1)} %param.9) | copy-start | bytes 786436

commit v8 on v7

--- a/solution.py
+++ b/solution.py
@@ -159,8 +159,8 @@
                             terms = [a + b for a, b in zip(terms[::2], terms[1::2], strict=True)]
                         totals += terms
                     north, south = totals
-                    line_ref[pl.ds(first + x, 8, stride=lines)] = north + south
-                    line_ref[pl.ds(maps + first + x, 8, stride=lines)] = north - south
+                    line_ref[pl.ds(first + x, 8, stride=lines)] = north
+                    line_ref[pl.ds(maps + first + x, 8, stride=lines)] = south
             gathered = line_ref[: band * lines]
             for piece in range(1, 8 // band):
                 gathered = gathered + line_ref[piece * band * lines : (piece + 1) * band * lines]
@@ -200,7 +200,7 @@
         cycle = lane // lines % band
         is_first = cycle == 0
         is_last = cycle == band - 1
-        mirror = jnp.where(lane // maps % 2 == 0, 1.0, -1.0)
+        south = lane // maps % 2 == 1
 
         single = []
         for b in range(blocks):
@@ -216,6 +216,9 @@
 
         def moved(value, shift):
             return pltpu.roll(value, shift % LANES, 1)
+
+        def opposite(value, shift=0):
+            return jnp.where(south, moved(value, shift + maps), moved(value, shift - maps))
 
         folded = []
         for b in range(0, blocks, 2):
@@ -231,14 +234,17 @@
             below_swapped = jnp.where(is_last, down, down_swapped)
             if b + 2 == blocks:
                 equator = is_last & ~lower
-                below = jnp.where(equator, mirror * here, below)
-                below_swapped = jnp.where(equator, mirror * swapped, below_swapped)
-            folded.append(
+                below = jnp.where(equator, opposite(here), below)
+                below_swapped = jnp.where(equator, opposite(here, half), below_swapped)
+            fourier = (
                 aux_ref[0] * here
                 + aux_ref[1] * (above + below)
                 + aux_ref[2] * swapped
                 + aux_ref[3] * (above_swapped + below_swapped)
             )
+            fourier = fourier.astype(jnp.bfloat16).astype(jnp.float32)
+            other = opposite(fourier)
+            folded.append(jnp.where(south, other - fourier, fourier + other))
         folded = jnp.concatenate(folded, axis=0).astype(jnp.bfloat16)
 
         row = iota((blocks * owned, depth), 0)

time: 17.4 us -> 17.5 us (level)
  no operation moved by 1% of the time
where the time goes in v8:
time: 17.5 us; the launch traced here: 17.3 us
  blocking collectives  14.5 us (83%)
  Pallas kernels  2.69 us (15%)
    all_to_all x1, blocking collectives, local(): lax.all_to_all(partial, ('blk', 'lblk'), split_axis=0, concat_axis=0, til...  14.5 us
    pallas_call x1, Pallas kernels, local(): pl.pallas_call(legendre_kernel(maps, band, owned, blocks, copies, degrees...  1.27 us
    pallas_call x1, Pallas kernels, local(): pl.pallas_call(table_kernel(band, quarter, ring, owned, chunk), out_shape...  0.96 us
    pallas_call x1, Pallas kernels, local(): pl.pallas_call(fourier_kernel(maps, band, pieces, owned, copies, chunk, c...  0.46 us

profile of v8, /device:TPU:0, one launch (start us, length us, event | category | flops | bytes accessed | tf_op | source)
XLA Modules:
  0.0 17.3 jit_solution(6616092046906033362)
XLA Ops:
  0.0 0.0 copy-start
  0.0 1.0 %tables.1 = (bf16[256,128]{1,0:T(8,128)(2,1)S(1)}, bf16[1,128,128]{2,1,0:T(8,128)(2,1)S(1)}, f32[1,128,128]{2,1,0:T(8,128)S(1)}, f32[5,8,128]{2,1,0:T(8,128)S(1)}) custom-call(s32[2,4]{1,0:T(2,128)} %start_ref.1, s32[2,4]{1,0:T(2,128)} %count_ref.1, s32[32]{0:T(128)} %modes_ref.1, s32[1,1,32]{2,1,0:T(1,128)} %bitcast.18), custom_call_target="tpu_custom_call" | custom-call | flops 1000000000 | bytes 4000000 | tf_op jit(solution)/shard_map/tables/pallas_call | solution.py:324
  1.0 0.1 copy-done
  1.1 0.0 copy-start.1
  1.1 0.5 %fourier.1 = f32[128,128]{1,0:T(8,128)S(1)} custom-call(bf16[2048,128]{1,0:T(8,128)(2,1)S(1)} %bitcast.14, bf16[256,128]{1,0:T(8,128)(2,1)S(1)} %get-tuple-element.9.mask_ref, bf16[1,128,128]{2,1,0:T(8,128)(2,1)S(1)} %get-tuple-element.10.table_ref, f32[1,128,128]{2,1,0:T(8,128)S(1)} %get-tuple-element.11.turn_ref), custom_call_target="tpu_custom_call" | custom-call | tf_op jit(solution)/shard_map/fourier/pallas_call | solution.py:338
  1.5 14.5 %all_to_all.5 = f32[32,4,128]{2,1,0:T(4,128)S(1)} all-to-all(f32[32,4,128]{2,1,0:T(4,128)S(1)} %bitcast.16), channel_id=1, replica_groups=mesh['blk'=8,'lblk'=4] {'blk','lblk'}, dimensions={0} | all-to-all | bytes 131072 | tf_op jit(solution)/shard_map/all_to_all | solution.py:348
  16.1 0.0 copy-done.1
  16.1 1.3 %legendre.1 = f32[512,128]{1,0:T(8,128)} custom-call(f32[128,128]{1,0:T(8,128)S(1)} %bitcast.17, f32[5,8,128]{2,1,0:T(8,128)S(1)} %get-tuple-element.12.aux_ref, bf16[32,4,1024]{2,1,0:T(4,128)(2,1)S(1)} %bitcast.15), custom_call_target="tpu_custom_call" | custom-call | tf_op jit(solution)/shard_map/legendre/pallas_call | solution.py:352
Async XLA Ops:
  0.0 1.1 %copy-start = (bf16[8,2,4,4096]{3,2,1,0:T(4,128)(2,1)S(1)}, bf16[8,2,4,4096]{3,2,1,0:T(4,128)(2,1)}, u32[]{:S(2)}) copy-start(bf16[8,2,4,4096]{3,2,1,0:T(4,128)(2,1)} %param.5) | copy-start | bytes 1572868
  1.1 15.0 %copy-start.1 = (bf16[4,8,4,1024]{3,2,1,0:T(4,128)(2,1)S(1)}, bf16[4,8,4,1024]{3,2,1,0:T(4,128)(2,1)}, u32[]{:S(2)}) copy-start(bf16[4,8,4,1024]{3,2,1,0:T(4,128)(2,1)} %param.9) | copy-start | bytes 786436

commit v9 on v8

--- a/solution.py
+++ b/solution.py
@@ -273,28 +273,28 @@
                 jnp.broadcast_to(line_ref[lines + i : lines + i + 1], (8, depth)),
             )
             weights.append(jnp.where(mine, value, 0.0))
-        weights = jnp.concatenate(weights, axis=0).astype(jnp.bfloat16)
-        sums = jnp.dot(weights, legendre_ref[...].reshape(depth, degrees), preferred_element_type=jnp.float32)
+        weights = jnp.concatenate(
+            [jnp.concatenate(weights[:maps], axis=0), jnp.concatenate(weights[maps:], axis=0)], axis=1
+        ).astype(jnp.bfloat16)
 
         mode = aux_ref[4].astype(jnp.int32)
-        degree = lax.axis_index("lblk") * degrees + lane
+        degree = lax.axis_index("lblk") * degrees + iota((8, degrees), 1)
+        mode = jnp.concatenate([mode] * columns, axis=1)
+        inside = degree >= mode
         even = ((degree + mode) & 1) == 0
-        beyond = degree - mode
+        given = legendre_ref[...].reshape(depth, degrees)
+        height = depth // owned
+        rows = []
+        for keep in (inside & even, inside & ~even):
+            keep = jnp.where(keep, 1.0, 0.0)
+            for s in range(owned):
+                factor = jnp.broadcast_to(keep[s : s + 1], (height, degrees)).astype(jnp.bfloat16)
+                rows.append(given[s * height : (s + 1) * height] * factor)
+        sums = jnp.dot(weights, jnp.concatenate(rows, axis=0), preferred_element_type=jnp.float32)
         for j in range(0, columns, 2):
-            inside = [beyond >= -(j + i) * LANES for i in range(2)]
             for x in range(maps):
-                near, far = (
-                    jnp.where(
-                        inside[i],
-                        jnp.where(
-                            even,
-                            sums[x * 8 : x * 8 + 8, (j + i) * LANES : (j + i + 1) * LANES],
-                            sums[(maps + x) * 8 : (maps + x) * 8 + 8, (j + i) * LANES : (j + i + 1) * LANES],
-                        ),
-                        0.0,
-                    )
-                    for i in range(2)
-                )
+                near = sums[x * 8 : x * 8 + 8, j * LANES : (j + 1) * LANES]
+                far = sums[x * 8 : x * 8 + 8, (j + 1) * LANES : (j + 2) * LANES]
                 at = (x * 2 * columns + j) * owned
                 out_ref[pl.ds(at, 8)] = jnp.where(lower, near, pltpu.roll(far, owned, 0))
                 at += columns * owned

time: 17.5 us -> 17.5 us (level)
  no operation moved by 1% of the time
where the time goes in v9:
time: 17.5 us; the launch traced here: 17.3 us
  blocking collectives  14.5 us (83%)
  Pallas kernels  2.66 us (15%)
    all_to_all x1, blocking collectives, local(): lax.all_to_all(partial, ('blk', 'lblk'), split_axis=0, concat_axis=0, til...  14.5 us
    pallas_call x1, Pallas kernels, local(): pl.pallas_call(legendre_kernel(maps, band, owned, blocks, copies, degrees...  1.25 us
    pallas_call x1, Pallas kernels, local(): pl.pallas_call(table_kernel(band, quarter, ring, owned, chunk), out_shape...  0.96 us
    pallas_call x1, Pallas kernels, local(): pl.pallas_call(fourier_kernel(maps, band, pieces, owned, copies, chunk, c...  0.46 us

profile of v9, /device:TPU:0, one launch (start us, length us, event | category | flops | bytes accessed | tf_op | source)
XLA Modules:
  0.0 17.3 jit_solution(9504680681252015446)
XLA Ops:
  0.0 0.0 copy-start
  0.0 1.0 %tables.1 = (bf16[256,128]{1,0:T(8,128)(2,1)S(1)}, bf16[1,128,128]{2,1,0:T(8,128)(2,1)S(1)}, f32[1,128,128]{2,1,0:T(8,128)S(1)}, f32[5,8,128]{2,1,0:T(8,128)S(1)}) custom-call(s32[2,4]{1,0:T(2,128)} %start_ref.1, s32[2,4]{1,0:T(2,128)} %count_ref.1, s32[32]{0:T(128)} %modes_ref.1, s32[1,1,32]{2,1,0:T(1,128)} %bitcast.18), custom_call_target="tpu_custom_call" | custom-call | flops 1000000000 | bytes 4000000 | tf_op jit(solution)/shard_map/tables/pallas_call | solution.py:324
  1.0 0.1 copy-done
  1.1 0.0 copy-start.1
  1.1 0.5 %fourier.1 = f32[128,128]{1,0:T(8,128)S(1)} custom-call(bf16[2048,128]{1,0:T(8,128)(2,1)S(1)} %bitcast.14, bf16[256,128]{1,0:T(8,128)(2,1)S(1)} %get-tuple-element.9.mask_ref, bf16[1,128,128]{2,1,0:T(8,128)(2,1)S(1)} %get-tuple-element.10.table_ref, f32[1,128,128]{2,1,0:T(8,128)S(1)} %get-tuple-element.11.turn_ref), custom_call_target="tpu_custom_call" | custom-call | tf_op jit(solution)/shard_map/fourier/pallas_call | solution.py:338
  1.5 14.5 %all_to_all.5 = f32[32,4,128]{2,1,0:T(4,128)S(1)} all-to-all(f32[32,4,128]{2,1,0:T(4,128)S(1)} %bitcast.16), channel_id=1, replica_groups=mesh['blk'=8,'lblk'=4] {'blk','lblk'}, dimensions={0} | all-to-all | bytes 131072 | tf_op jit(solution)/shard_map/all_to_all | solution.py:348
  16.1 0.0 copy-done.1
  16.1 1.2 %legendre.1 = f32[512,128]{1,0:T(8,128)} custom-call(f32[128,128]{1,0:T(8,128)S(1)} %bitcast.17, f32[5,8,128]{2,1,0:T(8,128)S(1)} %get-tuple-element.12.aux_ref, bf16[32,4,1024]{2,1,0:T(4,128)(2,1)S(1)} %bitcast.15), custom_call_target="tpu_custom_call" | custom-call | tf_op jit(solution)/shard_map/legendre/pallas_call | solution.py:352
Async XLA Ops:
  0.0 1.1 %copy-start = (bf16[8,2,4,4096]{3,2,1,0:T(4,128)(2,1)S(1)}, bf16[8,2,4,4096]{3,2,1,0:T(4,128)(2,1)}, u32[]{:S(2)}) copy-start(bf16[8,2,4,4096]{3,2,1,0:T(4,128)(2,1)} %param.5) | copy-start | bytes 1572868
  1.1 15.0 %copy-start.1 = (bf16[4,8,4,1024]{3,2,1,0:T(4,128)(2,1)S(1)}, bf16[4,8,4,1024]{3,2,1,0:T(4,128)(2,1)}, u32[]{:S(2)}) copy-start(bf16[4,8,4,1024]{3,2,1,0:T(4,128)(2,1)} %param.9) | copy-start | bytes 786436

commit v10 on v9

--- a/solution.py
+++ b/solution.py
@@ -159,8 +159,8 @@
                             terms = [a + b for a, b in zip(terms[::2], terms[1::2], strict=True)]
                         totals += terms
                     north, south = totals
-                    line_ref[pl.ds(first + x, 8, stride=lines)] = north
-                    line_ref[pl.ds(maps + first + x, 8, stride=lines)] = south
+                    line_ref[pl.ds(first + x, 8, stride=lines)] = north + south
+                    line_ref[pl.ds(maps + first + x, 8, stride=lines)] = north - south
             gathered = line_ref[: band * lines]
             for piece in range(1, 8 // band):
                 gathered = gathered + line_ref[piece * band * lines : (piece + 1) * band * lines]
@@ -200,7 +200,7 @@
         cycle = lane // lines % band
         is_first = cycle == 0
         is_last = cycle == band - 1
-        south = lane // maps % 2 == 1
+        mirror = jnp.where(lane // maps % 2 == 0, 1.0, -1.0)
 
         single = []
         for b in range(blocks):
@@ -216,9 +216,6 @@
 
         def moved(value, shift):
             return pltpu.roll(value, shift % LANES, 1)
-
-        def opposite(value, shift=0):
-            return jnp.where(south, moved(value, shift + maps), moved(value, shift - maps))
 
         folded = []
         for b in range(0, blocks, 2):
@@ -234,17 +231,14 @@
             below_swapped = jnp.where(is_last, down, down_swapped)
             if b + 2 == blocks:
                 equator = is_last & ~lower
-                below = jnp.where(equator, opposite(here), below)
-                below_swapped = jnp.where(equator, opposite(here, half), below_swapped)
-            fourier = (
+                below = jnp.where(equator, mirror * here, below)
+                below_swapped = jnp.where(equator, mirror * swapped, below_swapped)
+            folded.append(
                 aux_ref[0] * here
                 + aux_ref[1] * (above + below)
                 + aux_ref[2] * swapped
                 + aux_ref[3] * (above_swapped + below_swapped)
             )
-            fourier = fourier.astype(jnp.bfloat16).astype(jnp.float32)
-            other = opposite(fourier)
-            folded.append(jnp.where(south, other - fourier, fourier + other))
         folded = jnp.concatenate(folded, axis=0).astype(jnp.bfloat16)
 
         row = iota((blocks * owned, depth), 0)

time: 17.5 us -> 17.4 us (level)
  no operation moved by 1% of the time
where the time goes in v10:
time: 17.4 us; the launch traced here: 17.2 us
  blocking collectives  14.5 us (83%)
  Pallas kernels  2.59 us (15%)
    all_to_all x1, blocking collectives, local(): lax.all_to_all(partial, ('blk', 'lblk'), split_axis=0, concat_axis=0, til...  14.5 us
    pallas_call x1, Pallas kernels, local(): pl.pallas_call(legendre_kernel(maps, band, owned, blocks, copies, degrees...  1.17 us
    pallas_call x1, Pallas kernels, local(): pl.pallas_call(table_kernel(band, quarter, ring, owned, chunk), out_shape...  0.96 us
    pallas_call x1, Pallas kernels, local(): pl.pallas_call(fourier_kernel(maps, band, pieces, owned, copies, chunk, c...  0.46 us

profile of v10, /device:TPU:0, one launch (start us, length us, event | category | flops | bytes accessed | tf_op | source)
XLA Modules:
  0.0 17.2 jit_solution(4620204383723120087)
XLA Ops:
  0.0 0.0 copy-start
  0.0 1.0 %tables.1 = (bf16[256,128]{1,0:T(8,128)(2,1)S(1)}, bf16[1,128,128]{2,1,0:T(8,128)(2,1)S(1)}, f32[1,128,128]{2,1,0:T(8,128)S(1)}, f32[5,8,128]{2,1,0:T(8,128)S(1)}) custom-call(s32[2,4]{1,0:T(2,128)} %start_ref.1, s32[2,4]{1,0:T(2,128)} %count_ref.1, s32[32]{0:T(128)} %modes_ref.1, s32[1,1,32]{2,1,0:T(1,128)} %bitcast.18), custom_call_target="tpu_custom_call" | custom-call | flops 1000000000 | bytes 4000000 | tf_op jit(solution)/shard_map/tables/pallas_call | solution.py:318
  1.0 0.1 copy-done
  1.1 0.0 copy-start.1
  1.1 0.5 %fourier.1 = f32[128,128]{1,0:T(8,128)S(1)} custom-call(bf16[2048,128]{1,0:T(8,128)(2,1)S(1)} %bitcast.14, bf16[256,128]{1,0:T(8,128)(2,1)S(1)} %get-tuple-element.9.mask_ref, bf16[1,128,128]{2,1,0:T(8,128)(2,1)S(1)} %get-tuple-element.10.table_ref, f32[1,128,128]{2,1,0:T(8,128)S(1)} %get-tuple-element.11.turn_ref), custom_call_target="tpu_custom_call" | custom-call | tf_op jit(solution)/shard_map/fourier/pallas_call | solution.py:332
  1.5 14.5 %all_to_all.5 = f32[32,4,128]{2,1,0:T(4,128)S(1)} all-to-all(f32[32,4,128]{2,1,0:T(4,128)S(1)} %bitcast.16), channel_id=1, replica_groups=mesh['blk'=8,'lblk'=4] {'blk','lblk'}, dimensions={0} | all-to-all | bytes 131072 | tf_op jit(solution)/shard_map/all_to_all | solution.py:342
  16.1 0.0 copy-done.1
  16.1 1.2 %legendre.1 = f32[512,128]{1,0:T(8,128)} custom-call(f32[128,128]{1,0:T(8,128)S(1)} %bitcast.17, f32[5,8,128]{2,1,0:T(8,128)S(1)} %get-tuple-element.12.aux_ref, bf16[32,4,1024]{2,1,0:T(4,128)(2,1)S(1)} %bitcast.15), custom_call_target="tpu_custom_call" | custom-call | tf_op jit(solution)/shard_map/legendre/pallas_call | solution.py:346
Async XLA Ops:
  0.0 1.1 %copy-start = (bf16[8,2,4,4096]{3,2,1,0:T(4,128)(2,1)S(1)}, bf16[8,2,4,4096]{3,2,1,0:T(4,128)(2,1)}, u32[]{:S(2)}) copy-start(bf16[8,2,4,4096]{3,2,1,0:T(4,128)(2,1)} %param.5) | copy-start | bytes 1572868
  1.1 15.0 %copy-start.1 = (bf16[4,8,4,1024]{3,2,1,0:T(4,128)(2,1)S(1)}, bf16[4,8,4,1024]{3,2,1,0:T(4,128)(2,1)}, u32[]{:S(2)}) copy-start(bf16[4,8,4,1024]{3,2,1,0:T(4,128)(2,1)} %param.9) | copy-start | bytes 786436
